TPU v7x, 256 devices: a whole 4x4x8 slice. The times are simulated.
256 devices in a mesh: dp: 16 (over x_lo, z), space: 16 (over x_hi, y, core).
Axes of the slice: x: 4 (x_hi: 2, x_lo: 2; x = x_hi * 2 + x_lo), y: 4, z: 8, core: 2. Of those that a mesh axis runs over, the one named last changes fastest.
Arguments:
- volume_in: bfloat16 [16, 16, 16, 64, 128], P('dp', 'space'), may hold values from -6 to 6
- hidden_act: bfloat16 [16, 16, 32, 64, 128], P('dp', 'space'), may hold values from -6 to 6
- out_cot: bfloat16 [16, 16, 32, 64, 128], P('dp', 'space'), may hold values from -6 to 6
- kernel_one: bfloat16 [3, 3, 3, 16, 32], replicated, may hold values from -0.3125 to 0.3125
- kernel_two: bfloat16 [3, 3, 3, 32, 32], replicated, may hold values from -0.21875 to 0.21875
- grad_bucket: float32 [256, 524288], P(('dp', 'space')), may hold values from -1 to 1
Outputs:
- grad_input: bfloat16 [16, 16, 16, 64, 128], P('dp', 'space')
- grad_kernel_one: float32 [3, 3, 3, 16, 32], replicated
- grad_kernel_two: float32 [3, 3, 3, 32, 32], replicated
- bucket_sum: float32 [524288], replicated
All inputs are finite; a program needn't handle non-finite values.
Results may differ from a plain program's by a relative error of at most 0.013.
Values may be sent and summed in bfloat16 or wider, within the bound.
A program may use at most 128 MiB of HBM per device.

v0:
```python
import math

import jax
import jax.numpy as jnp
from jax import lax
from jax.sharding import PartitionSpec as P


def extended(value, sides, width):
    for axis, dim in sides:
        count, length = (lax.axis_size(axis), value.shape[dim])
        up = [(i, (i + 1) % count) for i in range(count - 1)]
        down = [(j, i) for i, j in up]
        last = lax.slice_in_dim(value, length - width, length, axis=dim)
        leading = lax.slice_in_dim(value, 0, width, axis=dim)
        before = lax.ppermute(last, axis, up)
        after = lax.ppermute(leading, axis, down)
        value = jnp.concatenate([before, value, after], axis=dim)
    return value


def convolve_planar(field, kernel):
    numbers = lax.ConvDimensionNumbers(
        lhs_spec=(0, 2, 1, 3, 4), rhs_spec=(4, 3, 0, 1, 2), out_spec=(0, 2, 1, 3, 4)
    )
    return lax.conv_general_dilated(
        field,
        kernel,
        (1, 1, 1),
        ((0, 0), (1, 1), (1, 1)),
        dimension_numbers=numbers,
        preferred_element_type=jnp.float32,
    )


def flipped(kernel):
    return jnp.swapaxes(kernel[::-1, ::-1, ::-1], 3, 4)


def kernel_terms(haloed, cotan):
    padded = jnp.pad(haloed, ((0, 0), (0, 0), (0, 0), (1, 1), (1, 1)))
    depth_cells, width_x, width_y = (cotan.shape[1], cotan.shape[3], cotan.shape[4])
    planes = []
    for along_z in range(3):
        for along_x in range(3):
            for along_y in range(3):
                window = padded[
                    :,
                    along_z : along_z + depth_cells,
                    :,
                    along_x : along_x + width_x,
                    along_y : along_y + width_y,
                ]
                planes.append(
                    jnp.einsum("nzcxy,nzdxy->cd", window, cotan, preferred_element_type=jnp.float32)
                )
    return jnp.stack(planes).reshape((3, 3, 3) + planes[0].shape)


def per_device(volume_in, hidden_act, out_cot, kernel_one, kernel_two, grad_bucket):
    haloed_vol, haloed_act, haloed_cot = (
        extended(volume_in, (("space", 1),), 1),
        extended(hidden_act, (("space", 1),), 1),
        extended(out_cot, (("space", 1),), 1),
    )
    act_grad = convolve_planar(haloed_cot, flipped(kernel_two))
    slope = jnp.where(hidden_act > 0, 1.0, 0.2).astype(jnp.float32)
    pre_grad = (act_grad * slope).astype(jnp.bfloat16)
    haloed_pre = extended(pre_grad, (("space", 1),), 1)
    grad_input = convolve_planar(haloed_pre, flipped(kernel_one)).astype(jnp.bfloat16)
    local_two = kernel_terms(haloed_act, out_cot)
    local_one = kernel_terms(haloed_vol, pre_grad)
    count = (
        volume_in.shape[0]
        * lax.axis_size("dp")
        * volume_in.shape[1]
        * lax.axis_size("space")
        * volume_in.shape[3]
        * volume_in.shape[4]
    )
    scale = 1.0 / math.sqrt(count)
    bucket_row = grad_bucket[0]
    total_one, total_two, bucket_sum = lax.psum((local_one, local_two, bucket_row), ("dp", "space"))
    return (grad_input, total_one * scale, total_two * scale, bucket_sum)


def solution(mesh):
    in_specs = (
        P("dp", "space", None, None, None),
        P("dp", "space", None, None, None),
        P("dp", "space", None, None, None),
        P(),
        P(),
        P(("dp", "space"), None),
    )
    out_specs = (P("dp", "space", None, None, None), P(), P(), P())
    return jax.shard_map(
        per_device, mesh=mesh, in_specs=in_specs, out_specs=out_specs, check_vma=False
    )
```

profile of v0, /device:TPU:1, one launch (start us, length us, event | category | flops | bytes accessed | tf_op | source)
XLA Modules:
  0.0 404.8 jit_solution(18215120016548208796)
XLA Ops:
  7.2 1.2 copy.236
  8.5 4.6 %collective-permute-start.4 = (bf16[1,1,16,64,128]{4,2,3,1,0:T(8,128)(2,1)S(1)}, bf16[1,1,16,64,128]{4,2,3,1,0:T(8,128)(2,1)S(1)}, u32[]{:S(2)}, u32[]{:S(2)}) collective-permute-start(bf16[1,1,16,64,128]{4,2,3,1,0:T(8,128)(2,1)S(1)} %copy.236), channel_id=1, source_target_pairs={{0,1},{1,2},{2,3},{3,4},{4,5},{5,6},{6,7},{7,8},{8,9},{9,10},{10,1... | collective-permute-start | bytes 786440 | tf_op jit(solution)/shard_map/ppermute | solution.py:16
  13.1 1.9 collective-permute-start.5
  15.0 1.9 collective-permute-start.1
  16.9 3.6 collective-permute-start
  20.6 2.2 copy.266
  22.8 1.9 collective-permute-start.7
  24.7 2.5 copy.223
  27.2 2.5 copy.228
  29.7 1.2 copy.252
  30.9 3.6 collective-permute-start.6
  34.6 1.3 copy.243
  35.9 0.7 copy-done.8
  36.6 1.3 copy.261
  37.9 2.7 select_maximum_fusion.2
  40.6 3.3 copy.224
  43.9 3.3 copy.222
  47.3 2.3 maximum_bitcast_fusion
  49.6 2.4 pad.10
  52.0 9.9 %copy.226 = bf16[3,32,64,1,8,17]{1,4,5,2,0,3:T(8,128)(2,1)} copy(bf16[3,32,64,1,8,17]{2,1,5,4,0,3:T(8,128)(2,1)} %bitcast.499) | data formatting | bytes 3342336 | tf_op jit(solution)/shard_map/conv_general_dilated | solution.py:26
  61.9 1.4 slice.208
  63.3 11.4 %broadcast_select_fusion = f32[1,64,8,17,32]{4,2,3,1,0:T(8,128)} fusion(pred[8,17]{0,1:T(8,128)(4,1)S(1)} %copy-done.15, bf16[3,3,3,32,32]{4,3,2,1,0:T(8,128)(2,1)S(1)} %copy-done, bf16[3,32,64,1,7,2]{1,4,5,2,0,3:T(8,128)(2,1)S(1)} %slice.208, bf16[3,32,64,1,8,17]{1,4,5,2,0,3:T(8,128)(2,1)} %copy.226), kind=kOutput, calls=%fused_computation.38 | convolution fusion | flops 482164736 | bytes 3012744 | tf_op jit(solution)/shard_map/conv_general_dilated | solution.py:26
  74.7 5.3 %copy.227 = f32[1,64,8,17,32]{1,4,3,2,0:T(8,128)} copy(f32[1,64,8,17,32]{4,2,3,1,0:T(8,128)} %broadcast_select_fusion) | data formatting | bytes 2228224 | tf_op jit(solution)/shard_map/conv_general_dilated | solution.py:26
  80.0 2.2 fusion.28
  82.2 1.9 copy.229
  84.1 1.9 collective-permute-start.3
  86.0 3.8 collective-permute-start.2
  89.8 1.6 copy.239
  99.2 3.3 select_maximum_fusion
  103.0 0.5 fusion.59
  104.5 1.5 fusion.56
  109.8 0.7 fusion.47
  114.3 1.5 fusion.38
  117.8 0.8 copy-done.12
  119.2 92.4 %psum.21 = f32[3,3,3,16,32]{4,3,2,1,0:T(8,128)S(1)} all-reduce(f32[3,3,3,16,32]{4,3,2,1,0:T(8,128)S(1)} %bitcast.535), channel_id=1, replica_groups=mesh['dp'=16,'space'=16] {'dp','space'}, use_global_device_ids=true, to_apply=%region_0.1 | all-reduce | flops 13824 | bytes 110592 | tf_op jit(solution)/shard_map/psum | solution.py:83
  211.6 0.7 broadcast_multiply_fusion.1
  212.3 2.5 copy.232
  214.8 3.3 copy.231
  218.1 2.0 maximum_bitcast_fusion.1
  220.1 0.6 pad.12
  220.8 8.0 %copy.234 = bf16[3,32,64,1,8,17]{1,4,5,2,0,3:T(8,128)(2,1)} copy(bf16[3,32,64,1,8,17]{2,1,5,4,0,3:T(8,128)(2,1)S(1)} %bitcast.498) | data formatting | bytes 3342336 | tf_op jit(solution)/shard_map/conv_general_dilated | solution.py:26
  228.8 1.4 slice.210
  230.1 9.9 %fusion.8 = bf16[1,64,8,17,16]{4,2,3,1,0:T(8,128)(2,1)S(1)} fusion(bf16[3,3,3,16,32]{4,3,2,1,0:T(8,128)(2,1)S(1)} %copy-done.14, bf16[3,32,64,1,7,2]{1,4,5,2,0,3:T(8,128)(2,1)S(1)} %slice.210, bf16[3,32,64,1,8,17]{1,4,5,2,0,3:T(8,128)(2,1)} %copy.234), kind=kOutput, calls=%fused_computation.12 | convolution fusion | flops 243744768 | bytes 2149376 | tf_op jit(solution)/shard_map/conv_general_dilated | solution.py:26
  240.0 2.0 copy.235
  242.3 1.1 copy.297
  243.5 149.4 %all-reduce.5.cloned.1.call-done = (f32[3,3,3,32,32]{4,3,2,1,0:T(8,128)}, f32[524288]{0:T(1024)}) async-done(((f32[3,3,3,32,32]{4,3,2,1,0:T(8,128)}, f32[524288]{0:T(1024)}), (f32[3,3,3,32,32]{4,3,2,1,0:T(8,128)}, f32[524288]{0:T(1024)})) %all-reduce.5.cloned.1.call-update) | async-done | bytes 2207760 | tf_op jit(solution)/shard_map/psum | solution.py:83
  392.9 1.8 broadcast_multiply_fusion
  394.7 3.0 copy.409
  (92 shorter events, 19.7 us)
Async XLA Ops:
  7.2 56.1 %copy-start = (bf16[3,3,3,32,32]{4,3,2,1,0:T(8,128)(2,1)S(1)}, bf16[3,3,3,32,32]{4,3,2,1,0:T(8,128)(2,1)}, u32[]{:S(2)}) copy-start(bf16[3,3,3,32,32]{4,3,2,1,0:T(8,128)(2,1)} %param.10) | copy-start | bytes 165892
  7.2 22.6 %copy-start.9 = (bf16[1,1,16,64,128]{4,3,2,1,0:T(8,128)(2,1)S(1)}, bf16[1,1,16,64,128]{4,3,2,1,0:T(8,128)(2,1)}, u32[]{:S(2)}) copy-start(bf16[1,1,16,64,128]{4,3,2,1,0:T(8,128)(2,1)} %param.6) | copy-start | bytes 786436
  7.2 20.0 %copy-start.2 = (bf16[1,1,32,64,128]{4,3,2,1,0:T(8,128)(2,1)S(1)}, bf16[1,1,32,64,128]{4,3,2,1,0:T(8,128)(2,1)}, u32[]{:S(2)}) copy-start(bf16[1,1,32,64,128]{4,3,2,1,0:T(8,128)(2,1)} %param.7) | copy-start | bytes 1572868
  7.2 385.7 %all-reduce.5.cloned.1.call-start = ((), (), s32[]{:S(2)}) async-start(), calls=%async_computation | async-start | bytes 5079040 | tf_op jit(solution)/shard_map/psum | solution.py:83
  8.5 27.5 %copy-start.10 = (bf16[1,1,16,64,128]{4,2,3,1,0:T(8,128)(2,1)}, bf16[1,1,16,64,128]{4,2,3,1,0:T(8,128)(2,1)S(1)}, u32[]{:S(2)}) copy-start(bf16[1,1,16,64,128]{4,2,3,1,0:T(8,128)(2,1)S(1)} %copy.236) | copy-start | bytes 786436
  8.5 22.5 %collective-permute-start.4 = (bf16[1,1,16,64,128]{4,2,3,1,0:T(8,128)(2,1)S(1)}, bf16[1,1,16,64,128]{4,2,3,1,0:T(8,128)(2,1)S(1)}, u32[]{:S(2)}, u32[]{:S(2)}) collective-permute-start(bf16[1,1,16,64,128]{4,2,3,1,0:T(8,128)(2,1)S(1)} %copy.236), channel_id=1, source_target_pairs={{0,1},{1,2},{2,3},{3,4},{4,5},{5,6},{6,7},{7,8},{8,9},{9,10},{10,1... | collective-permute-start | bytes 786440 | tf_op jit(solution)/shard_map/ppermute | solution.py:16
  13.1 22.8 %collective-permute-start.5 = (bf16[1,1,16,64,128]{4,2,3,1,0:T(8,128)(2,1)S(1)}, bf16[1,1,16,64,128]{4,2,3,1,0:T(8,128)(2,1)S(1)}, u32[]{:S(2)}, u32[]{:S(2)}) collective-permute-start(bf16[1,1,16,64,128]{4,2,3,1,0:T(8,128)(2,1)S(1)} %copy.236), channel_id=1, source_target_pairs={{1,0},{2,1},{3,2},{4,3},{5,4},{6,5},{7,6},{8,7},{9,8},{10,9},{11,1... | collective-permute-start | bytes 786440 | tf_op jit(solution)/shard_map/ppermute | solution.py:17
  15.0 25.6 %collective-permute-start.1 = (bf16[1,1,32,64,128]{4,3,2,1,0:T(8,128)(2,1)}, bf16[1,1,32,64,128]{4,3,2,1,0:T(8,128)(2,1)}, u32[]{:S(2)}, u32[]{:S(2)}) collective-permute-start(bf16[1,1,32,64,128]{4,3,2,1,0:T(8,128)(2,1)} %param.8), channel_id=1, source_target_pairs={{1,0},{2,1},{3,2},{4,3},{5,4},{6,5},{7,6},{8,7},{9,8},{10,9},{11,1... | collective-permute-start | bytes 1572872 | tf_op jit(solution)/shard_map/ppermute | solution.py:17
  16.9 27.0 %collective-permute-start = (bf16[1,1,32,64,128]{4,3,2,1,0:T(8,128)(2,1)}, bf16[1,1,32,64,128]{4,3,2,1,0:T(8,128)(2,1)}, u32[]{:S(2)}, u32[]{:S(2)}) collective-permute-start(bf16[1,1,32,64,128]{4,3,2,1,0:T(8,128)(2,1)} %param.8), channel_id=1, source_target_pairs={{0,1},{1,2},{2,3},{3,4},{4,5},{5,6},{6,7},{7,8},{8,9},{9,10},{10,1... | collective-permute-start | bytes 1572872 | tf_op jit(solution)/shard_map/ppermute | solution.py:16
  22.8 76.4 %collective-permute-start.7 = (bf16[1,1,32,64,128]{4,2,3,1,0:T(8,128)(2,1)}, bf16[1,1,32,64,128]{4,2,3,1,0:T(8,128)(2,1)}, u32[]{:S(2)}, u32[]{:S(2)}) collective-permute-start(bf16[1,1,32,64,128]{4,2,3,1,0:T(8,128)(2,1)} %copy.266), channel_id=1, source_target_pairs={{1,0},{2,1},{3,2},{4,3},{5,4},{6,5},{7,6},{8,7},{9,8},{10,9},{11,1... | collective-permute-start | bytes 1572872 | tf_op jit(solution)/shard_map/ppermute | solution.py:17
  30.9 5.0 %copy-start.7 = (bf16[1,1,16,64,128]{4,2,3,1,0:T(8,128)(2,1)}, bf16[1,1,16,64,128]{4,2,3,1,0:T(8,128)(2,1)S(1)}, u32[]{:S(2)}) copy-start(bf16[1,1,16,64,128]{4,2,3,1,0:T(8,128)(2,1)S(1)} %collective-permute-done.4) | copy-start | bytes 786436
  30.9 68.3 %collective-permute-start.6 = (bf16[1,1,32,64,128]{4,2,3,1,0:T(8,128)(2,1)}, bf16[1,1,32,64,128]{4,2,3,1,0:T(8,128)(2,1)}, u32[]{:S(2)}, u32[]{:S(2)}) collective-permute-start(bf16[1,1,32,64,128]{4,2,3,1,0:T(8,128)(2,1)} %copy.266), channel_id=1, source_target_pairs={{0,1},{1,2},{2,3},{3,4},{4,5},{5,6},{6,7},{7,8},{8,9},{9,10},{10,1... | collective-permute-start | bytes 1572872 | tf_op jit(solution)/shard_map/ppermute | solution.py:16
  35.9 0.7 copy-start.8
  52.0 11.3 %copy-start.15 = (pred[8,17]{0,1:T(8,128)(4,1)S(1)}, pred[8,17]{0,1:T(8,128)(4,1)}, u32[]{:S(2)}) copy-start(pred[8,17]{0,1:T(8,128)(4,1)} %constant.29) | copy-start | bytes 412
  84.1 128.2 %collective-permute-start.3 = (bf16[1,1,32,64,128]{4,3,2,1,0:T(8,128)(2,1)}, bf16[1,1,32,64,128]{4,3,2,1,0:T(8,128)(2,1)}, u32[]{:S(2)}, u32[]{:S(2)}) collective-permute-start(bf16[1,1,32,64,128]{4,3,2,1,0:T(8,128)(2,1)} %copy.229), channel_id=1, source_target_pairs={{1,0},{2,1},{3,2},{4,3},{5,4},{6,5},{7,6},{8,7},{9,8},{10,9},{11,1... | collective-permute-start | bytes 1572872 | tf_op jit(solution)/shard_map/ppermute | solution.py:17
  86.0 128.8 %collective-permute-start.2 = (bf16[1,1,32,64,128]{4,3,2,1,0:T(8,128)(2,1)}, bf16[1,1,32,64,128]{4,3,2,1,0:T(8,128)(2,1)}, u32[]{:S(2)}, u32[]{:S(2)}) collective-permute-start(bf16[1,1,32,64,128]{4,3,2,1,0:T(8,128)(2,1)} %copy.229), channel_id=1, source_target_pairs={{0,1},{1,2},{2,3},{3,4},{4,5},{5,6},{6,7},{7,8},{8,9},{9,10},{10,1... | collective-permute-start | bytes 1572872 | tf_op jit(solution)/shard_map/ppermute | solution.py:16
  91.4 1.2 copy-start.6
  93.0 2.4 copy-start.5
  95.8 2.4 copy-start.4
  98.6 4.0 copy-start.11
  107.4 2.4 copy-start.3
  117.8 0.8 copy-start.12
  220.8 9.3 %copy-start.14 = (bf16[3,3,3,16,32]{4,3,2,1,0:T(8,128)(2,1)S(1)}, bf16[3,3,3,16,32]{4,3,2,1,0:T(8,128)(2,1)}, u32[]{:S(2)}) copy-start(bf16[3,3,3,16,32]{4,3,2,1,0:T(8,128)(2,1)} %param.9) | copy-start | bytes 82948
  230.1 11.9 %copy-start.13 = (pred[8,17]{1,0:T(8,128)(4,1)S(1)}, pred[8,17]{1,0:T(8,128)(4,1)}, u32[]{:S(2)}) copy-start(pred[8,17]{1,0:T(8,128)(4,1)} %constant.27) | copy-start | bytes 412
  242.3 155.5 %copy-start.1 = (bf16[3,3,3,32,32]{4,3,2,1,0:T(8,128)(2,1)S(1)}, bf16[3,3,3,32,32]{4,3,2,1,0:T(8,128)(2,1)}, u32[]{:S(2)}) copy-start(bf16[3,3,3,32,32]{4,3,2,1,0:T(8,128)(2,1)} %param.10) | copy-start | bytes 165892
Sparse Core Ops, SparseCore 0:
  119.0 273.8 all-reduce.4
where the time goes:
time: 411 us; the launch traced here: 405 us
  waiting for transfers between devices  149 us (36%)
  blocking collectives  92.4 us (22%)
  local copies, waits for them, and re-layouts  64.9 us (16%)
  matrix products  44.8 us (11%)
  starting transfers between devices  23.4 us (6%)
  other arithmetic  15.3 us (4%)
  between operations  14.6 us (4%)
    psum x1, waiting for transfers between devices, per_device(): lax.psum((local_one, local_two, bucket_row), ('dp', 'space'))  149 us
    psum x1, blocking collectives, per_device(): lax.psum((local_one, local_two, bucket_row), ('dp', 'space'))  92.4 us
    conv_general_dilated x6, local copies, waits for them, and re-layouts, convolve_planar(): lax.conv_general_dilated(field, kernel, (1, 1, 1), ((0, 0), (1, 1), (1, 1...  27.9 us
    dot_general x54, matrix products, kernel_terms(): jnp.einsum('nzcxy,nzdxy->cd', window, cotan, preferred_element_type=jnp.f...  23.5 us
    conv_general_dilated x2, matrix products, convolve_planar(): lax.conv_general_dilated(field, kernel, (1, 1, 1), ((0, 0), (1, 1), (1, 1...  21.3 us
    ppermute x4, starting transfers between devices, extended(): before = lax.ppermute(last, axis, up)  15.7 us
    unnamed x38, local copies, waits for them, and re-layouts  14.2 us
    concatenate x4, other arithmetic, extended(): value = jnp.concatenate([before, value, after], axis=dim)  10.3 us
  transfers between devices with their start and end apart: 9, of which 1 were waited for; matrix products, arithmetic and copies ran while one was open for 29% of the time, Pallas kernels for 0%

commit v1 on v0

v1 whole, which is shorter than its diff:
```python
import functools
import math

import jax
import jax.numpy as jnp
from jax import lax
from jax.experimental import pallas as pl
from jax.experimental.pallas import tpu as pltpu
from jax.sharding import PartitionSpec as P

MESH = pl.DeviceIdType.MESH
F32 = jnp.float32
BF16 = jnp.bfloat16
LANES = 128
GROWS = 512


def landed(ref, sem):
    pltpu.make_async_copy(ref, ref, sem).wait()


def shifted(value, step):
    width = value.shape[-1]
    lane = lax.broadcasted_iota(jnp.int32, value.shape, value.ndim - 1)
    if step < 0:
        return jnp.where(lane >= 1, pltpu.roll(value, 1, value.ndim - 1), 0.0)
    return jnp.where(lane < width - 1, pltpu.roll(value, width - 1, value.ndim - 1), 0.0)


def relaid(raw, start, count):
    return jnp.transpose(raw[:, pl.ds(start, count), :].astype(F32), (1, 0, 2))


def weights(kernel, out, channels):
    for j in range(3):
        for k in range(3):
            pieces = [kernel[(2 - p) * 9 + (2 - j) * 3 + (2 - k)].astype(F32) for p in range(3)]
            row = (j * 3 + k) * channels
            out[row : row + channels, :] = jnp.concatenate(pieces, axis=1).astype(BF16)


def convolve(field, weight, total, width_x, channels):
    rows = 3 * channels
    total[0:2] = jnp.zeros((2, rows, LANES), F32)

    @pl.loop(0, width_x // 2)
    def _(step):
        x = step * 2
        pair = jnp.concatenate([field[x], field[x + 1]], axis=1)
        product = jnp.dot(weight[...], pair, preferred_element_type=F32)
        first, second = product[:, :LANES], product[:, LANES:]
        total[x] += first[2 * rows :]
        total[x + 1] += first[rows : 2 * rows] + second[2 * rows :]
        total[x + 2] = first[:rows] + second[rows : 2 * rows]
        total[x + 3] = second[:rows]


def gathered(total, x, channels):
    value = total[x + 1]
    return (
        value[channels : 2 * channels]
        + shifted(value[:channels], -1)
        + shifted(value[2 * channels :], 1)
    )


def kernel_terms(field, planes, out, first, width_x, channels):
    rows = 9 * channels
    depth = planes.shape[1]
    unroll = 4
    out[first : first + rows, :] = jnp.zeros((rows, LANES), F32)

    @pl.loop(0, width_x // unroll)
    def _(step):
        x = step * unroll
        left = jnp.concatenate(
            [field[pl.ds(x + u, 3)].reshape(rows, LANES) for u in range(unroll)], axis=1
        )
        right = jnp.concatenate([planes[x + u] for u in range(unroll)], axis=1)
        out[first : first + rows, :depth] += lax.dot_general(
            left, right, (((1,), (1,)), ((), ())), preferred_element_type=F32
        )


def kernel(
    n, m, scale,
    vol_hbm, act_hbm, cot_hbm, one_hbm, two_hbm, bucket_hbm,
    gin_hbm, g1_hbm, g2_hbm, bsum_hbm,
    raw_vol, raw_act, raw_cot, one_v, two_v, bucket,
    cotf, actf, volf, pref, acc_two, acc_one, gin, w_one, w_two,
    s0, r0, s1, r1, s2, r2, gath,
    gpart, gsend, grecv, gx, gfull, g1_v, g2_v,
    load_sem, out_sem, halo_send, halo_recv, b_send, b_recv, g_send, g_recv,
):
    c1, width_x, width_y = raw_act.shape
    c0, c2 = raw_vol.shape[0], raw_cot.shape[0]
    dp = lax.axis_index("dp")
    sp = lax.axis_index("space")
    half = m // 2
    core, pos = lax.rem(sp, 2), sp // 2
    rows = bucket.shape[0]
    h = rows // 2
    q = h // max(half, 1)
    e = q // n
    gr = GROWS // m

    def in_space(other):
        return (dp, other)

    def in_dp(other):
        return (other, sp)

    def remote(src, dst, send, recv, device):
        return pltpu.make_async_remote_copy(
            src_ref=src, dst_ref=dst, send_sem=send, recv_sem=recv, device_id=device, device_id_type=MESH
        )

    if n * m > 1:
        barrier = pltpu.get_barrier_semaphore()

        @pl.loop(1, m)
        def _(o):
            pl.semaphore_signal(barrier, inc=1, device_id=in_space(lax.rem(sp + o, m)), device_id_type=MESH)

        @pl.loop(1, n)
        def _(o):
            pl.semaphore_signal(barrier, inc=1, device_id=in_dp(lax.rem(dp + o, n)), device_id_type=MESH)

    loads = [
        pltpu.make_async_copy(src, dst, load_sem.at[i])
        for i, (src, dst) in enumerate(
            (
                (cot_hbm, raw_cot), (bucket_hbm, bucket), (act_hbm, raw_act),
                (two_hbm, two_v), (vol_hbm, raw_vol), (one_hbm, one_v),
            )
        )
    ]
    for load in loads:
        load.start()
    block = 16

    loads[0].wait()

    @pl.loop(0, width_x // block)
    def _(step):
        x = step * block
        cotf[pl.ds(x, block), c2 : 2 * c2, :] = relaid(raw_cot, x, block).astype(BF16)

    if n * m > 1:
        pl.semaphore_wait(barrier, m - 1 + n - 1)

    def exchange(field, depth, index):
        own = field.at[:, depth : 2 * depth, :]
        lower, upper = field.at[:, 0:depth, :], field.at[:, 2 * depth : 3 * depth, :]
        up = remote(own, lower, halo_send.at[index, 0], halo_recv.at[index, 0], in_space(lax.rem(sp + 1, m)))
        down = remote(own, upper, halo_send.at[index, 1], halo_recv.at[index, 1], in_space(lax.rem(sp + m - 1, m)))

        @pl.when(sp < m - 1)
        def _():
            up.start()

        @pl.when(sp > 0)
        def _():
            down.start()

        def arrive():
            @pl.when(sp > 0)
            def _():
                landed(lower, halo_recv.at[index, 0])

            @pl.when(sp < m - 1)
            def _():
                landed(upper, halo_recv.at[index, 1])

        def sent():
            @pl.when(sp < m - 1)
            def _():
                landed(own, halo_send.at[index, 0])

            @pl.when(sp > 0)
            def _():
                landed(own, halo_send.at[index, 1])

        return arrive, sent

    def blank(field, depth):
        @pl.when(sp == 0)
        def _():
            @pl.loop(0, width_x)
            def _(x):
                field[x, 0:depth, :] = jnp.zeros((depth, LANES), BF16)

        @pl.when(sp == m - 1)
        def _():
            @pl.loop(0, width_x)
            def _(x):
                field[x, 2 * depth : 3 * depth, :] = jnp.zeros((depth, LANES), BF16)

    cot_arrive, cot_sent = exchange(cotf, c2, 0)
    blank(cotf, c2)
    blank(pref, c1)

    part = 256

    loads[1].wait()
    partner = in_space(sp + 1 - 2 * core)
    if m > 1:
        far = (1 - core) * h
        near = core * h

        @pl.loop(0, h // part)
        def _(t):
            s0[pl.ds(t * part, part), :] = bucket[pl.ds(pl.multiple_of(far + t * part, part), part), :].astype(BF16)

        remote(s0, r0, b_send.at[0], b_recv.at[0], partner).start()

    def spread(raw, field, channels):
        zero = jnp.zeros((3 * channels, LANES), BF16)
        field[0] = zero
        field[width_x + 1] = zero

        @pl.loop(0, width_x // block)
        def _(step):
            x = step * block
            value = relaid(raw, x, block).reshape(block * channels, LANES)
            for k in range(3):
                moved = value if k == 1 else shifted(value, k - 1)
                field[pl.ds(x + 1, block), k * channels : (k + 1) * channels, :] = moved.astype(BF16).reshape(
                    block, channels, LANES
                )

    loads[2].wait()
    spread(raw_act, actf, c1)
    loads[3].wait()
    weights(two_v, w_two, c1)

    if m > 1:
        landed(r0, b_recv.at[0])

        @pl.loop(0, h // part)
        def _(t):
            at = pl.ds(pl.multiple_of(near + t * part, part), part)
            value = bucket[at, :] + r0[pl.ds(t * part, part), :].astype(F32)
            bucket[at, :] = value
            s1[pl.ds(t * part, part), :] = value.astype(BF16)

        @pl.loop(1, half)
        def _(o):
            other = lax.rem(pos + o, half)
            remote(
                s1.at[pl.ds(pl.multiple_of(other * q, q), q), :], r1.at[o - 1],
                b_send.at[1], b_recv.at[1], in_space(other * 2 + core),
            ).start()

    loads[4].wait()
    spread(raw_vol, volf, c0)
    loads[5].wait()
    weights(one_v, w_one, c0)

    if m > 1:
        cot_arrive()
    convolve(cotf, w_two, acc_two, width_x, c1)

    @pl.loop(0, width_x // 2)
    def _(step):
        for u in range(2):
            x = step * 2 + u
            slope = jnp.where(actf[x + 1, c1 : 2 * c1, :].astype(F32) > 0, 1.0, 0.2)
            pref[x, c1 : 2 * c1, :] = (gathered(acc_two, x, c1) * slope).astype(BF16)

    pre_arrive, pre_sent = exchange(pref, c1, 1)

    mine = core * h + pos * q
    if m > 1:
        if half > 1:
            landed(r1, b_recv.at[1])
        own = pl.ds(pl.multiple_of(mine, q), q)
        value = bucket[own, :]
        for o in range(1, half):
            value = value + r1[o - 1].astype(F32)
        bucket[own, :] = value
        s2[...] = value.astype(BF16)

        @pl.loop(1, n)
        def _(o):
            other = lax.rem(dp + o, n)
            remote(
                s2.at[pl.ds(pl.multiple_of(other * e, e), e), :], r2.at[o - 1],
                b_send.at[2], b_recv.at[2], in_dp(other),
            ).start()

    kernel_terms(actf, cotf, gpart, 0, width_x, c1)

    if m > 1:
        landed(r2, b_recv.at[2])
        start = pl.multiple_of(mine + dp * e, e)
        value = bucket[pl.ds(start, e), :]
        for o in range(1, n):
            value = value + r2[o - 1].astype(F32)
        own_rows = gath.at[pl.ds(start, e), :]
        own_rows[...] = value.astype(BF16)

        @pl.loop(1, n)
        def _(o):
            remote(own_rows, own_rows, b_send.at[3], b_recv.at[3], in_dp(lax.rem(dp + o, n))).start()

    if m > 1:
        pre_arrive()
    kernel_terms(volf, pref, gpart, 9 * c1, width_x, c0)
    used = 9 * (c1 + c0)
    gpart[used:, :] = jnp.zeros((GROWS - used, LANES), F32)

    if m > 1:
        gsend[...] = gpart[...].astype(gsend.dtype)

        @pl.loop(1, m)
        def _(o):
            other = lax.rem(sp + o, m)
            remote(
                gsend.at[pl.ds(pl.multiple_of(other * gr, gr), gr), :], grecv.at[o - 1],
                g_send.at[0], g_recv.at[0], in_space(other),
            ).start()

        landed(gath.at[pl.ds(0, (n - 1) * e), :], b_recv.at[3])
        own_part = gath.at[pl.ds(pl.multiple_of(mine, q), q), :]

        @pl.loop(1, half)
        def _(o):
            other = lax.rem(pos + o, half)
            remote(own_part, own_part, b_send.at[4], b_recv.at[4], in_space(other * 2 + core)).start()

    convolve(pref, w_one, acc_one, width_x, c0)

    @pl.loop(0, width_x // 4)
    def _(step):
        for u in range(4):
            x = step * 4 + u
            gin[x] = gathered(acc_one, x, c0).astype(BF16)

    gin_out = pltpu.make_async_copy(gin, gin_hbm, out_sem.at[0])
    gin_out.start()

    if m > 1:
        landed(grecv, g_recv.at[0])
        value = gpart[pl.ds(pl.multiple_of(sp * gr, gr), gr), :]
        for o in range(1, m):
            value = value + grecv[o - 1].astype(F32)
        gx[dp] = value.astype(gx.dtype)

        @pl.loop(1, n)
        def _(o):
            remote(gx.at[dp], gx.at[dp], g_send.at[1], g_recv.at[1], in_dp(lax.rem(dp + o, n))).start()

        if half > 1:
            landed(gath.at[pl.ds(0, (half - 1) * q), :], b_recv.at[4])
        own_half = gath.at[pl.ds(pl.multiple_of(near, h), h), :]
        remote(own_half, own_half, b_send.at[5], b_recv.at[5], partner).start()

        landed(gx.at[pl.ds(0, n - 1)], g_recv.at[1])
        value = gx[0].astype(F32)
        for d in range(1, n):
            value = value + gx[d].astype(F32)
        own_rows_g = gfull.at[pl.ds(pl.multiple_of(sp * gr, gr), gr), :]
        own_rows_g[...] = (value * scale).astype(gfull.dtype)

        @pl.loop(1, m)
        def _(o):
            remote(own_rows_g, own_rows_g, g_send.at[2], g_recv.at[2], in_space(lax.rem(sp + o, m))).start()

        landed(gath.at[pl.ds(0, h), :], b_recv.at[5])
    bsum_out = pltpu.make_async_copy(gath, bsum_hbm, out_sem.at[1])
    bsum_out.start()
    if m > 1:
        landed(gfull.at[pl.ds(0, (m - 1) * gr), :], g_recv.at[2])

    for j in range(3):
        for k in range(3):
            for p in range(3):
                at = (2 - p) * 9 + j * 3 + k
                row = (j * 3 + k) * c1
                g2_v[at] = gfull[row : row + c1, p * c2 : (p + 1) * c2].astype(F32)
                row = 9 * c1 + (j * 3 + k) * c0
                g1_v[at] = gfull[row : row + c0, p * c1 : (p + 1) * c1].astype(F32)
    g2_out = pltpu.make_async_copy(g2_v, g2_hbm, out_sem.at[2])
    g1_out = pltpu.make_async_copy(g1_v, g1_hbm, out_sem.at[3])
    g2_out.start()
    g1_out.start()

    if m > 1:
        cot_sent()
        pre_sent()
        landed(s0, b_send.at[0])
        if half > 1:
            landed(r1, b_send.at[1])
            landed(gath.at[pl.ds(0, (half - 1) * q), :], b_send.at[4])
        landed(r2, b_send.at[2])
        landed(gath.at[pl.ds(0, (n - 1) * e), :], b_send.at[3])
        landed(gath.at[pl.ds(0, h), :], b_send.at[5])
        landed(grecv, g_send.at[0])
        landed(gx.at[pl.ds(0, n - 1)], g_send.at[1])
        landed(gfull.at[pl.ds(0, (m - 1) * gr), :], g_send.at[2])
    gin_out.wait()
    bsum_out.wait()
    g2_out.wait()
    g1_out.wait()


def call(n, m, scale, vol, act, cot, one, two, bucket):
    c0, width_x, width_y = vol.shape
    c1, c2 = act.shape[0], cot.shape[0]
    rows = bucket.shape[0]
    half = max(m // 2, 1)
    h = rows // 2
    q = h // half
    e = q // n
    gr = GROWS // m
    wire = BF16
    vmem = pltpu.VMEM
    scratch = [
        vmem((c0, width_x, width_y), BF16), vmem((c1, width_x, width_y), BF16), vmem((c2, width_x, width_y), BF16),
        vmem((27, c0, c1), BF16), vmem((27, c1, c2), BF16), vmem((rows, LANES), F32),
        vmem((width_x, 3 * c2, LANES), BF16), vmem((width_x + 2, 3 * c1, LANES), BF16),
        vmem((width_x + 2, 3 * c0, LANES), BF16), vmem((width_x, 3 * c1, LANES), BF16),
        vmem((width_x + 2, 3 * c1, LANES), F32), vmem((width_x + 2, 3 * c0, LANES), F32),
        vmem((width_x, c0, LANES), BF16),
        vmem((9 * c0, 3 * c1), BF16), vmem((9 * c1, 3 * c2), BF16),
        vmem((h, LANES), BF16), vmem((h, LANES), BF16), vmem((h, LANES), BF16),
        vmem((max(half - 1, 1), q, LANES), BF16), vmem((q, LANES), BF16), vmem((max(n - 1, 1), e, LANES), BF16),
        vmem((rows, LANES), BF16),
        vmem((GROWS, LANES), F32), vmem((GROWS, LANES), wire), vmem((max(m - 1, 1), gr, LANES), wire),
        vmem((n, gr, LANES), wire), vmem((GROWS, LANES), wire),
        vmem((27, c0, c1), F32), vmem((27, c1, c2), F32),
        pltpu.SemaphoreType.DMA((6,)), pltpu.SemaphoreType.DMA((4,)),
        pltpu.SemaphoreType.DMA((2, 2)), pltpu.SemaphoreType.DMA((2, 2)),
        pltpu.SemaphoreType.DMA((6,)), pltpu.SemaphoreType.DMA((6,)),
        pltpu.SemaphoreType.DMA((3,)), pltpu.SemaphoreType.DMA((3,)),
    ]
    hbm = pl.BlockSpec(memory_space=pltpu.HBM)
    cells = width_x * width_y
    return pl.pallas_call(
        functools.partial(kernel, n, m, scale),
        out_shape=(
            jax.ShapeDtypeStruct((width_x, c0, width_y), BF16),
            jax.ShapeDtypeStruct((27, c0, c1), F32),
            jax.ShapeDtypeStruct((27, c1, c2), F32),
            jax.ShapeDtypeStruct((rows, LANES), BF16),
        ),
        in_specs=[hbm] * 6,
        out_specs=(hbm,) * 4,
        scratch_shapes=scratch,
        compiler_params=pltpu.CompilerParams(
            collective_id=0 if n * m > 1 else None, has_side_effects=True, vmem_limit_bytes=64 << 20
        ),
        cost_estimate=pl.CostEstimate(
            flops=4 * 27 * cells * c1 * (c0 + c2), bytes_accessed=8 << 20, transcendentals=0
        ),
    )(vol, act, cot, one, two, bucket)


def per_device(n, m, volume_in, hidden_act, out_cot, kernel_one, kernel_two, grad_bucket):
    c0, width_x, width_y = volume_in.shape[2:]
    c1 = hidden_act.shape[2]
    scale = 1.0 / math.sqrt(volume_in.shape[0] * n * volume_in.shape[1] * m * width_x * width_y)
    gin, g1, g2, bsum = call(
        n, m, scale,
        volume_in[0, 0], hidden_act[0, 0], out_cot[0, 0],
        kernel_one.reshape((27,) + kernel_one.shape[3:]), kernel_two.reshape((27,) + kernel_two.shape[3:]),
        grad_bucket.reshape(-1, LANES),
    )
    gin = jnp.transpose(gin, (1, 0, 2))[None, None]
    return (
        gin, g1.reshape(kernel_one.shape), g2.reshape(kernel_two.shape), bsum.astype(F32).reshape(-1),
    )


def solution(mesh):
    fields = P("dp", "space", None, None, None)
    return jax.shard_map(
        functools.partial(per_device, mesh.shape["dp"], mesh.shape["space"]),
        mesh=mesh,
        in_specs=(fields, fields, fields, P(), P(), P(("dp", "space"), None)),
        out_specs=(fields, P(), P(), P()),
        check_vma=False,
    )
```

time: 411 us -> 70.2 us (0.17); the launches traced: 405 us -> 70 us
  waiting for transfers between devices: 149 us -> 0 us
  blocking collectives: 92.4 us -> 0 us
  Pallas kernels: 0 us -> 63.4 us
  local copies, waits for them, and re-layouts: 64.9 us -> 3.24 us
  matrix products: 44.8 us -> 0 us
  starting transfers between devices: 23.4 us -> 0 us
  between operations: 14.6 us -> 0.66 us
  other arithmetic: 15.3 us -> 2.68 us
    psum x1 -> x0, waiting for transfers between devices: 149 us -> none  [per_device(): lax.psum((local_one, local_two, bucket_row), ('dp', 'space'))]
    psum x1 -> x0, blocking collectives: 92.4 us -> none  [per_device(): lax.psum((local_one, local_two, bucket_row), ('dp', 'space'))]
    pallas_call x0 -> x1, Pallas kernels: none -> 63.4 us  [call(): pl.pallas_call(functools.partial(kernel, n, m, scale), out_shape=(jax.Sha...]
    conv_general_dilated x6 -> x0, local copies, waits for them, and re-layouts: 27.9 us -> none  [convolve_planar(): lax.conv_general_dilated(field, kernel, (1, 1, 1), ((0, 0), (1, 1), (1, 1...]
    dot_general x54 -> x0, matrix products: 23.5 us -> none  [kernel_terms(): jnp.einsum('nzcxy,nzdxy->cd', window, cotan, preferred_element_type=jnp.f...]
    ppermute x8 -> x0, starting transfers between devices: 23.4 us -> none  [the longest x4 15.7 us: extended(): before = lax.ppermute(last, axis, up)]
    conv_general_dilated x2 -> x0, matrix products: 21.3 us -> none  [convolve_planar(): lax.conv_general_dilated(field, kernel, (1, 1, 1), ((0, 0), (1, 1), (1, 1...]
    ppermute x4 -> x0, local copies, waits for them, and re-layouts: 12.4 us -> none  [the longest x2 6.67 us: extended(): before = lax.ppermute(last, axis, up)]
  transfers between devices with their start and end apart: 9 -> 0, of which waited for: 1 -> 0; matrix products, arithmetic and copies ran while one was open for 29% -> 0% of each run, Pallas kernels for 0% -> 0%
where the time goes in v1:
time: 70.2 us; the launch traced here: 70 us
  Pallas kernels  63.4 us (90%)
  local copies, waits for them, and re-layouts  3.24 us (5%)
  other arithmetic  2.68 us (4%)
    pallas_call x1, Pallas kernels, call(): pl.pallas_call(functools.partial(kernel, n, m, scale), out_shape=(jax.Sha...  63.4 us
    unnamed x7, local copies, waits for them, and re-layouts  3.24 us
    reshape x1, other arithmetic, per_device(): bsum.astype(F32).reshape(-1)  2.68 us

profile of v1, /device:TPU:1, one launch (start us, length us, event | category | flops | bytes accessed | tf_op | source)
XLA Modules:
  0.0 70.0 jit_solution(1310331006826741365)
XLA Ops:
  0.6 63.4 %shard_map.93 = (bf16[64,16,128]{2,1,0:T(8,128)(2,1)}, f32[27,16,32]{2,1,0:T(8,128)}, f32[27,32,32]{2,1,0:T(8,128)}, bf16[4096,128]{1,0:T(8,128)(2,1)}) custom-call(bf16[16,64,128]{2,1,0:T(8,128)(2,1)} %bitcast.20, bf16[32,64,128]{2,1,0:T(8,128)(2,1)} %bitcast.18, bf16[32,64,128]{2,1,0:T(8,128)(2,1)} %bitcast.19, bf16[27,16,32]{2,1,0:T(8,128)(2,1)} %bitcast.22, ...), custom_call_target="tpu_custom_call" | custom-call | flops 1358954496 | bytes 8388608 | tf_op jit(solution)/shard_map/pallas_call | solution.py:440
  64.1 0.0 copy-start.1
  64.1 0.0 copy-start
  64.1 1.8 %copy.10 = bf16[1,1,16,64,128]{4,3,2,1,0:T(8,128)(2,1)} copy(bf16[1,1,16,64,128]{4,2,3,1,0:T(8,128)(2,1)} %bitcast.15) | data formatting | bytes 524288
  65.9 2.7 %bitcast_convert_fusion = f32[524288]{0:T(1024)} fusion(bf16[4096,128]{1,0:T(8,128)(2,1)} %get-tuple-element.11), kind=kLoop, calls=%fused_computation | loop fusion | flops 524288 | bytes 3145728 | tf_op jit(solution)/shard_map/reshape | solution.py:472
  68.6 0.0 copy-done.1
  68.6 0.7 copy.13
  69.2 0.0 copy-done
  69.3 0.8 %copy.14 = f32[3,3,3,32,32]{4,3,2,1,0:T(8,128)} copy(f32[3,3,3,32,32]{4,3,2,1,0:T(8,128)S(1)} %bitcast.14) | data formatting | bytes 221184
Async XLA Ops:
  64.1 4.5 %copy-start.1 = (f32[27,16,32]{2,1,0:T(8,128)S(1)}, f32[27,16,32]{2,1,0:T(8,128)}, u32[]{:S(2)}) copy-start(f32[27,16,32]{2,1,0:T(8,128)} %get-tuple-element.9) | copy-start | bytes 165892
  64.1 5.2 %copy-start = (f32[27,32,32]{2,1,0:T(8,128)S(1)}, f32[27,32,32]{2,1,0:T(8,128)}, u32[]{:S(2)}) copy-start(f32[27,32,32]{2,1,0:T(8,128)} %get-tuple-element.10) | copy-start | bytes 331780

commit v2 on v1

v2 whole, which is shorter than its diff:
```python
import functools
import math

import jax
import jax.numpy as jnp
from jax import lax
from jax.experimental import pallas as pl
from jax.experimental.pallas import tpu as pltpu
from jax.sharding import PartitionSpec as P

MESH = pl.DeviceIdType.MESH
F32 = jnp.float32
BF16 = jnp.bfloat16
LANES = 128
GROWS = 512
UNROLL = 16
COUNT = 8
VMEM_LIMIT = 40 << 20


def landed(ref, sem):
    pltpu.make_async_copy(ref, ref, sem).wait()


def shifted(value, step):
    width = value.shape[-1]
    lane = lax.broadcasted_iota(jnp.int32, value.shape, value.ndim - 1)
    if step < 0:
        return jnp.where(lane >= 1, pltpu.roll(value, 1, value.ndim - 1), 0.0)
    return jnp.where(lane < width - 1, pltpu.roll(value, width - 1, value.ndim - 1), 0.0)


def relaid(raw, start, count):
    return jnp.transpose(raw[:, pl.ds(start, count), :].astype(F32), (1, 0, 2))


def weights(kernel, out, channels):
    for k in range(3):
        pieces = [
            kernel[(2 - p) * 9 + (2 - j) * 3 + (2 - k)].astype(F32) for j in range(3) for p in range(3)
        ]
        out[k * channels : (k + 1) * channels, :] = jnp.concatenate(pieces, axis=1).astype(BF16)


def convolved(field, weight, x, count, channels):
    rows = weight.shape[1]
    columns = [field[pl.ds(x + u, 3)].reshape(rows, LANES) for u in range(count)]
    product = jnp.dot(weight[...], jnp.concatenate(columns, axis=1), preferred_element_type=F32)
    out = []
    for u in range(count):
        value = product[:, u * LANES : (u + 1) * LANES]
        out.append(
            value[channels : 2 * channels]
            + shifted(value[:channels], -1)
            + shifted(value[2 * channels :], 1)
        )
    return out


def kernel_terms(left, right, offset, out, first, low, high, unroll):
    rows = 3 * left.shape[1]
    depth = right.shape[1]

    @pl.loop(0, (high - low) // unroll)
    def _(step):
        x = low + step * unroll
        a = jnp.concatenate([left[pl.ds(x + u, 3)].reshape(rows, LANES) for u in range(unroll)], axis=1)
        b = jnp.concatenate([right[x + u + offset] for u in range(unroll)], axis=1)
        out[first : first + rows, :depth] += lax.dot_general(
            a, b, (((1,), (1,)), ((), ())), preferred_element_type=F32
        )


def kernel(
    n, m, scale,
    vol_hbm, act_hbm, cot_hbm, one_hbm, two_hbm, bucket_hbm,
    gin, gfull, gath,
    raw_vol, raw_act, raw_cot, one_v, two_v, bucket,
    cotf, actf, volf, pref, turned, w_one, w_two,
    r0, s1, r1, s2, r2,
    gpart, gsend, grecv, gx,
    load_sem, halo_send, halo_recv, b_send, b_recv, c_recv, g_send, g_recv,
):
    c1, width_x, width_y = raw_act.shape
    c0, c2 = raw_vol.shape[0], raw_cot.shape[0]
    dp = lax.axis_index("dp")
    sp = lax.axis_index("space")
    half = max(m // 2, 1)
    core, pos = lax.rem(sp, 2), sp // 2
    h = bucket.shape[0]
    q = h // half
    e = q // n
    gr = GROWS // m
    near, far = core * h, (1 - core) * h
    mine = near + pos * q
    partner = (dp, sp + 1 - 2 * core)

    def in_space(other):
        return (dp, other)

    def in_dp(other):
        return (other, sp)

    def remote(src, dst, send, recv, device):
        return pltpu.make_async_remote_copy(
            src_ref=src, dst_ref=dst, send_sem=send, recv_sem=recv, device_id=device, device_id_type=MESH
        )

    if n * m > 1:
        barrier = pltpu.get_barrier_semaphore()

        @pl.loop(1, m)
        def _(o):
            pl.semaphore_signal(barrier, inc=1, device_id=in_space(lax.rem(sp + o, m)), device_id_type=MESH)

        @pl.loop(1, n)
        def _(o):
            pl.semaphore_signal(barrier, inc=1, device_id=in_dp(lax.rem(dp + o, n)), device_id_type=MESH)

    loads = [
        pltpu.make_async_copy(src, dst, load_sem.at[i])
        for i, (src, dst) in enumerate(
            (
                (cot_hbm, raw_cot), (vol_hbm, raw_vol), (act_hbm, raw_act),
                (two_hbm, two_v), (one_hbm, one_v), (bucket_hbm.at[pl.ds(pl.multiple_of(near, h), h), :], bucket),
            )
        )
    ]
    for load in loads:
        load.start()
    block = 16

    for field in (cotf, actf, volf, pref):
        for slot in (0, width_x + 1):
            field[slot] = jnp.zeros(field.shape[1:], BF16)
    gpart[...] = jnp.zeros(gpart.shape, F32)

    def center(raw, field, channels):
        @pl.loop(0, width_x // block)
        def _(step):
            x = step * block
            field[pl.ds(x + 1, block), channels : 2 * channels, :] = relaid(raw, x, block).astype(BF16)

    def spread(raw, field, channels):
        @pl.loop(0, width_x // block)
        def _(step):
            x = step * block
            value = relaid(raw, x, block).reshape(block * channels, LANES)
            for k in range(3):
                moved = value if k == 1 else shifted(value, k - 1)
                field[pl.ds(x + 1, block), k * channels : (k + 1) * channels, :] = moved.astype(BF16).reshape(
                    block, channels, LANES
                )

    def planes(field, low, high):
        depth = field.shape[1] // 3
        return [field.at[low + 1 : high + 1, p * depth : (p + 1) * depth, :] for p in range(3)]

    def send_halo(field, low, high, index):
        lower, own, upper = planes(field, low, high)

        @pl.when(sp < m - 1)
        def _():
            remote(own, lower, halo_send.at[index, 0], halo_recv.at[index, 0], in_space(lax.rem(sp + 1, m))).start()

        @pl.when(sp > 0)
        def _():
            remote(own, upper, halo_send.at[index, 1], halo_recv.at[index, 1], in_space(lax.rem(sp + m - 1, m))).start()

    def have_halo(field, low, high, index):
        lower, own, upper = planes(field, low, high)

        @pl.when(sp > 0)
        def _():
            landed(lower, halo_recv.at[index, 0])

        @pl.when(sp < m - 1)
        def _():
            landed(upper, halo_recv.at[index, 1])

    def sent_halo(field, low, high, index):
        lower, own, upper = planes(field, low, high)

        @pl.when(sp < m - 1)
        def _():
            landed(own, halo_send.at[index, 0])

        @pl.when(sp > 0)
        def _():
            landed(own, halo_send.at[index, 1])

    def blank(field):
        depth = field.shape[1] // 3
        for edge, p in ((0, 0), (m - 1, 2)):

            @pl.when(sp == edge)
            def _():
                @pl.loop(1, width_x + 1)
                def _(x):
                    field[x, p * depth : (p + 1) * depth, :] = jnp.zeros((depth, LANES), BF16)

    pieces = 4
    length = width_x // pieces
    raw_cuts = [(c * length, (c + 1) * length) for c in range(pieces)]
    pre_cuts = [
        (max(low - COUNT, 0), high if c == pieces - 1 else high - COUNT) for c, (low, high) in enumerate(raw_cuts)
    ]

    loads[0].wait()
    center(raw_cot, cotf, c2)
    if n * m > 1:
        pl.semaphore_wait(barrier, m - 1 + n - 1)
        for c, (low, high) in enumerate(raw_cuts):
            send_halo(cotf, low, high, c)
        remote(bucket_hbm.at[pl.ds(pl.multiple_of(far, h), h), :], r0, b_send.at[0], b_recv.at[0], partner).start()
    blank(cotf)
    blank(volf)
    blank(pref)
    loads[1].wait()
    center(raw_vol, volf, c0)
    if n * m > 1:
        send_halo(volf, 0, width_x, 2 * pieces)
    loads[2].wait()
    spread(raw_act, actf, c1)
    loads[3].wait()
    weights(two_v, w_two, c1)
    loads[4].wait()
    weights(one_v, w_one, c0)
    loads[5].wait()

    part = min(256, h)
    if m > 1:
        landed(r0, b_recv.at[0])

        @pl.loop(0, h // part)
        def _(t):
            at = pl.ds(t * part, part)
            value = bucket[at, :] + r0[at, :]
            bucket[at, :] = value
            s1[at, :] = value.astype(BF16)

        @pl.loop(1, half)
        def _(o):
            other = lax.rem(pos + o, half)
            remote(
                s1.at[pl.ds(pl.multiple_of(other * q, q), q), :], r1.at[o - 1],
                b_send.at[1], b_recv.at[1], in_space(other * 2 + core),
            ).start()

    def third():
        if half > 1:
            landed(r1, b_recv.at[1])
        own = pl.ds(pl.multiple_of(pos * q, q), q)
        value = bucket[own, :]
        for o in range(1, half):
            value = value + r1[o - 1].astype(F32)
        bucket[own, :] = value
        s2[...] = value.astype(BF16)

        @pl.loop(1, n)
        def _(o):
            other = lax.rem(dp + o, n)
            remote(
                s2.at[pl.ds(pl.multiple_of(other * e, e), e), :], r2.at[o - 1],
                b_send.at[2], b_recv.at[2], in_dp(other),
            ).start()

    for c in range(pieces):
        low, high = pre_cuts[c]
        if m > 1:
            have_halo(cotf, *raw_cuts[c], c)

        @pl.loop(0, (high - low) // COUNT)
        def _(step):
            x = low + step * COUNT
            for u, value in enumerate(convolved(cotf, w_two, x, COUNT, c1)):
                slope = jnp.where(actf[x + u + 1, c1 : 2 * c1, :].astype(F32) > 0, 1.0, 0.2)
                value = (value * slope).astype(BF16)
                pref[x + u + 1, c1 : 2 * c1, :] = value
                wide = value.astype(F32)
                turned[x + u, :c1, :] = shifted(wide, 1).astype(BF16)
                turned[x + u, c1 : 2 * c1, :] = value
                turned[x + u, 2 * c1 :, :] = shifted(wide, -1).astype(BF16)

        if m > 1:
            send_halo(pref, low, high, pieces + c)
            if c == 2:
                third()
        kernel_terms(actf, cotf, 1, gpart, 0, *raw_cuts[c], UNROLL)

    if m > 1:
        have_halo(volf, 0, width_x, 2 * pieces)
    kernel_terms(volf, turned, 0, gpart, 9 * c1, 0, width_x, UNROLL)

    if m > 1:
        gsend[...] = gpart[...].astype(gsend.dtype)

        @pl.loop(1, m)
        def _(o):
            other = lax.rem(sp + o, m)
            remote(
                gsend.at[pl.ds(pl.multiple_of(other * gr, gr), gr), :], grecv.at[o - 1],
                g_send.at[0], g_recv.at[0], in_space(other),
            ).start()

        landed(r2, b_recv.at[2])
        value = bucket[pl.ds(pl.multiple_of(pos * q + dp * e, e), e), :]
        for o in range(1, n):
            value = value + r2[o - 1].astype(F32)
        own_rows = gath.at[pl.ds(pl.multiple_of(mine + dp * e, e), e), :]
        own_rows[...] = value.astype(BF16)

        @pl.loop(1, n)
        def _(o):
            remote(own_rows, own_rows, b_send.at[3], b_recv.at[3], in_dp(lax.rem(dp + o, n))).start()

    def second(low, high):
        @pl.loop(0, (high - low) // COUNT)
        def _(step):
            x = low + step * COUNT
            for u, value in enumerate(convolved(pref, w_one, x, COUNT, c0)):
                gin[x + u] = value.astype(BF16)

    if m > 1:
        for c in range(pieces):
            have_halo(pref, *pre_cuts[c], pieces + c)
    second(0, width_x)

    if m > 1:
        landed(grecv, g_recv.at[0])
        value = gpart[pl.ds(pl.multiple_of(sp * gr, gr), gr), :]
        for o in range(1, m):
            value = value + grecv[o - 1].astype(F32)
        gx[dp] = value.astype(gx.dtype)

        @pl.loop(1, n)
        def _(o):
            remote(gx.at[dp], gx.at[dp], g_send.at[1], g_recv.at[1], in_dp(lax.rem(dp + o, n))).start()

        def rows_of(chip):
            return gath.at[pl.ds(pl.multiple_of(near + chip * q, q), q), :]

        landed(gath.at[pl.ds(0, (n - 1) * e), :], b_recv.at[3])

        @pl.loop(1, half)
        def _(o):
            other = lax.rem(pos + o, half)
            remote(rows_of(pos), rows_of(pos), b_send.at[4], c_recv.at[o - 1], in_space(other * 2 + core)).start()

        remote(rows_of(pos), rows_of(pos), b_send.at[5], b_recv.at[5], partner).start()

        landed(gx.at[pl.ds(0, n - 1)], g_recv.at[1])
        value = gx[0].astype(F32)
        for d in range(1, n):
            value = value + gx[d].astype(F32)
        own_g = gfull.at[pl.ds(pl.multiple_of(sp * gr, gr), gr), :]
        own_g[...] = (value * scale).astype(gfull.dtype)

        @pl.loop(1, m)
        def _(o):
            remote(own_g, own_g, g_send.at[2], g_recv.at[2], in_space(lax.rem(sp + o, m))).start()

        @pl.loop(1, half)
        def _(o):
            chip = lax.rem(pos + half - o, half)
            landed(rows_of(chip), c_recv.at[o - 1])
            remote(rows_of(chip), rows_of(chip), b_send.at[5], b_recv.at[5], partner).start()

        landed(gfull.at[pl.ds(0, (m - 1) * gr), :], g_recv.at[2])
        landed(gath.at[pl.ds(0, h), :], b_recv.at[5])

        for c in range(pieces):
            sent_halo(cotf, *raw_cuts[c], c)
            sent_halo(pref, *pre_cuts[c], pieces + c)
        sent_halo(volf, 0, width_x, 2 * pieces)
        landed(r0, b_send.at[0])
        if half > 1:
            landed(r1, b_send.at[1])
            landed(gath.at[pl.ds(0, (half - 1) * q), :], b_send.at[4])
        landed(r2, b_send.at[2])
        landed(gath.at[pl.ds(0, (n - 1) * e), :], b_send.at[3])
        landed(gath.at[pl.ds(0, h), :], b_send.at[5])
        landed(grecv, g_send.at[0])
        landed(gx.at[pl.ds(0, n - 1)], g_send.at[1])
        landed(gfull.at[pl.ds(0, (m - 1) * gr), :], g_send.at[2])


def finish(gin, gfull, gath, gin_hbm, g1_hbm, g2_hbm, bsum_hbm, gin_v, g1_v, g2_v, bsum_v, sem):
    width_x, c0, _ = gin.shape
    c1, c2 = g2_v.shape[1:]
    rows = gath.shape[0]
    count = 8
    part = rows // count
    copies = []
    for t in range(count):
        at = pl.ds(t * part, part)
        bsum_v[at, :] = gath[at, :].astype(F32)
        copies.append(pltpu.make_async_copy(bsum_v.at[at, :], bsum_hbm.at[at, :], sem.at[t]))
        copies[-1].start()
    block = 16
    for t in range(width_x // block):
        at = pl.ds(t * block, block)
        gin_v[:, at, :] = jnp.transpose(gin[at].astype(F32), (1, 0, 2)).astype(BF16)
    copies.append(pltpu.make_async_copy(gin_v, gin_hbm, sem.at[count]))
    copies[-1].start()
    for j in range(3):
        for k in range(3):
            for p in range(3):
                row = (j * 3 + k) * c1
                g2_v[(2 - p) * 9 + j * 3 + k] = gfull[row : row + c1, p * c2 : (p + 1) * c2].astype(F32)
                row = 9 * c1 + (j * 3 + p) * c0
                g1_v[p * 9 + j * 3 + k] = gfull[row : row + c0, k * c1 : (k + 1) * c1].astype(F32)
    copies.append(pltpu.make_async_copy(g2_v, g2_hbm, sem.at[count + 1]))
    copies.append(pltpu.make_async_copy(g1_v, g1_hbm, sem.at[count + 2]))
    copies[-2].start()
    copies[-1].start()
    for copy in copies:
        copy.wait()


def call(n, m, scale, vol, act, cot, one, two, bucket):
    c0, width_x, width_y = vol.shape
    c1, c2 = act.shape[0], cot.shape[0]
    rows = bucket.shape[0]
    half = max(m // 2, 1)
    h = rows // 2
    q = h // half
    e = q // n
    gr = GROWS // m
    wire = BF16
    vmem = pltpu.VMEM
    dma = pltpu.SemaphoreType.DMA
    tall = width_x + 2
    scratch = [
        vmem((c0, width_x, width_y), BF16), vmem((c1, width_x, width_y), BF16), vmem((c2, width_x, width_y), BF16),
        vmem((27, c0, c1), BF16), vmem((27, c1, c2), BF16), vmem((h, LANES), F32),
        vmem((tall, 3 * c2, LANES), BF16), vmem((tall, 3 * c1, LANES), BF16),
        vmem((tall, 3 * c0, LANES), BF16), vmem((tall, 3 * c1, LANES), BF16),
        vmem((width_x, 3 * c1, LANES), BF16),
        vmem((3 * c0, 9 * c1), BF16), vmem((3 * c1, 9 * c2), BF16),
        vmem((h, LANES), F32), vmem((h, LANES), BF16),
        vmem((max(half - 1, 1), q, LANES), BF16), vmem((q, LANES), BF16), vmem((max(n - 1, 1), e, LANES), BF16),
        vmem((GROWS, LANES), F32), vmem((GROWS, LANES), wire), vmem((max(m - 1, 1), gr, LANES), wire),
        vmem((n, gr, LANES), wire),
        dma((6,)), dma((9, 2)), dma((9, 2)), dma((6,)), dma((6,)), dma((max(half - 1, 1),)), dma((3,)), dma((3,)),
    ]
    hbm = pl.BlockSpec(memory_space=pltpu.HBM)
    local = pl.BlockSpec(memory_space=pltpu.VMEM)
    cells = width_x * width_y
    operands = [pltpu.with_memory_space_constraint(v, pltpu.HBM) for v in (vol, act, cot, one, two, bucket)]
    gin, gfull, gath = pl.pallas_call(
        functools.partial(kernel, n, m, scale),
        out_shape=(
            jax.ShapeDtypeStruct((width_x, c0, width_y), BF16),
            jax.ShapeDtypeStruct((GROWS, LANES), wire),
            jax.ShapeDtypeStruct((rows, LANES), BF16),
        ),
        in_specs=[hbm] * 6,
        out_specs=(local,) * 3,
        scratch_shapes=scratch,
        compiler_params=pltpu.CompilerParams(
            collective_id=0 if n * m > 1 else None, has_side_effects=True, vmem_limit_bytes=VMEM_LIMIT
        ),
        cost_estimate=pl.CostEstimate(
            flops=4 * 27 * cells * c1 * (c0 + c2), bytes_accessed=8 << 20, transcendentals=0
        ),
    )(*operands)
    return pl.pallas_call(
        finish,
        out_shape=(
            jax.ShapeDtypeStruct((c0, width_x, width_y), BF16),
            jax.ShapeDtypeStruct((27, c0, c1), F32),
            jax.ShapeDtypeStruct((27, c1, c2), F32),
            jax.ShapeDtypeStruct((rows, LANES), F32),
        ),
        in_specs=[local] * 3,
        out_specs=(hbm,) * 4,
        scratch_shapes=[
            vmem((c0, width_x, width_y), BF16), vmem((27, c0, c1), F32), vmem((27, c1, c2), F32),
            vmem((rows, LANES), F32), dma((11,)),
        ],
        compiler_params=pltpu.CompilerParams(vmem_limit_bytes=VMEM_LIMIT),
        cost_estimate=pl.CostEstimate(flops=0, bytes_accessed=5 << 20, transcendentals=0),
    )(gin, gfull, gath)


def per_device(n, m, volume_in, hidden_act, out_cot, kernel_one, kernel_two, grad_bucket):
    width_x, width_y = volume_in.shape[3:]
    scale = 1.0 / math.sqrt(volume_in.shape[0] * n * volume_in.shape[1] * m * width_x * width_y)
    gin, g1, g2, bsum = call(
        n, m, scale,
        volume_in[0, 0], hidden_act[0, 0], out_cot[0, 0],
        kernel_one.reshape((27,) + kernel_one.shape[3:]), kernel_two.reshape((27,) + kernel_two.shape[3:]),
        grad_bucket.reshape(-1, LANES),
    )
    return (gin[None, None], g1.reshape(kernel_one.shape), g2.reshape(kernel_two.shape), bsum.reshape(-1))


def solution(mesh):
    fields = P("dp", "space", None, None, None)
    return jax.shard_map(
        functools.partial(per_device, mesh.shape["dp"], mesh.shape["space"]),
        mesh=mesh,
        in_specs=(fields, fields, fields, P(), P(), P(("dp", "space"), None)),
        out_specs=(fields, P(), P(), P()),
        check_vma=False,
    )
```

time: 70.2 us -> 53.4 us (0.76)
  Pallas kernels: 63.4 us -> 52.7 us
  local copies, waits for them, and re-layouts: 3.24 us -> 0 us
  other arithmetic: 2.68 us -> 0 us
    pallas_call x1, Pallas kernels: 63.4 us -> 50.9 us  [call(): pl.pallas_call(functools.partial(kernel, n, m, scale), out_shape=(jax.Sha...]
    unnamed x7 -> x0, local copies, waits for them, and re-layouts: 3.24 us -> none
    reshape x1 -> x0, other arithmetic: 2.68 us -> none  [per_device(): bsum.astype(F32).reshape(-1)]
    pallas_call x0 -> x1, Pallas kernels: none -> 1.76 us  [call(): pl.pallas_call(finish, out_shape=(jax.ShapeDtypeStruct((c0, width_x, widt...]
where the time goes in v2:
time: 53.4 us; the launch traced here: 53.3 us
  Pallas kernels  52.7 us (99%)
  between operations  0.64 us (1%)
    pallas_call x1, Pallas kernels, call(): pl.pallas_call(functools.partial(kernel, n, m, scale), out_shape=(jax.Sha...  50.9 us
    pallas_call x1, Pallas kernels, call(): pl.pallas_call(finish, out_shape=(jax.ShapeDtypeStruct((c0, width_x, widt...  1.76 us

profile of v2, /device:TPU:1, one launch (start us, length us, event | category | flops | bytes accessed | tf_op | source)
XLA Modules:
  0.0 53.3 jit_solution(11372999513040103757)
XLA Ops:
  0.6 50.9 %shard_map.93 = (bf16[64,16,128]{2,1,0:T(8,128)(2,1)S(1)}, bf16[512,128]{1,0:T(8,128)(2,1)S(1)}, bf16[4096,128]{1,0:T(8,128)(2,1)S(1)}) custom-call(bf16[16,64,128]{2,1,0:T(8,128)(2,1)} %bitcast.15, bf16[32,64,128]{2,1,0:T(8,128)(2,1)} %bitcast.12, bf16[32,64,128]{2,1,0:T(8,128)(2,1)} %bitcast.13, bf16[27,16,32]{2,1,0:T(8,128)(2,1)} %bitcast.19, ...), custom_call_target="tpu_custom_call" | custom-call | flops 1358954496 | bytes 8388608 | tf_op jit(solution)/shard_map/pallas_call | solution.py:451
  51.6 1.8 %shard_map.94 = (bf16[16,64,128]{2,1,0:T(8,128)(2,1)}, f32[27,16,32]{2,1,0:T(8,128)}, f32[27,32,32]{2,1,0:T(8,128)}, f32[4096,128]{1,0:T(8,128)}) custom-call(bf16[64,16,128]{2,1,0:T(8,128)(2,1)S(1)} %get-tuple-element.11.gin, bf16[512,128]{1,0:T(8,128)(2,1)S(1)} %get-tuple-element.12.gfull, bf16[4096,128]{1,0:T(8,128)(2,1)S(1)} %get-tuple-element.13.gath), custom_call_target="tpu_custom_call" | custom-call | bytes 5242880 | tf_op jit(solution)/shard_map/pallas_call | solution.py:468

commit v3 on v2

--- a/solution.py
+++ b/solution.py
@@ -15,6 +15,8 @@
 GROWS = 512
 UNROLL = 16
 COUNT = 8
+PARTS = 2
+TILE = 8
 VMEM_LIMIT = 40 << 20
 
 
@@ -88,11 +90,11 @@
     half = max(m // 2, 1)
     core, pos = lax.rem(sp, 2), sp // 2
     h = bucket.shape[0]
-    q = h // half
+    whole = h // PARTS
+    q = whole // half
     e = q // n
     gr = GROWS // m
     near, far = core * h, (1 - core) * h
-    mine = near + pos * q
     partner = (dp, sp + 1 - 2 * core)
 
     def in_space(other):
@@ -122,18 +124,13 @@
         for i, (src, dst) in enumerate(
             (
                 (cot_hbm, raw_cot), (vol_hbm, raw_vol), (act_hbm, raw_act),
-                (two_hbm, two_v), (one_hbm, one_v), (bucket_hbm.at[pl.ds(pl.multiple_of(near, h), h), :], bucket),
+                (two_hbm, two_v), (one_hbm, one_v), (bucket_hbm.at[pl.ds(near, h)], bucket),
             )
         )
     ]
     for load in loads:
         load.start()
     block = 16
-
-    for field in (cotf, actf, volf, pref):
-        for slot in (0, width_x + 1):
-            field[slot] = jnp.zeros(field.shape[1:], BF16)
-    gpart[...] = jnp.zeros(gpart.shape, F32)
 
     def center(raw, field, channels):
         @pl.loop(0, width_x // block)
@@ -206,69 +203,119 @@
         (max(low - COUNT, 0), high if c == pieces - 1 else high - COUNT) for c, (low, high) in enumerate(raw_cuts)
     ]
 
-    loads[0].wait()
-    center(raw_cot, cotf, c2)
+    def first(t):
+        at = t * whole
+        remote(
+            bucket_hbm.at[pl.ds(far + at, whole)], r0.at[pl.ds(at, whole)], b_send.at[t, 0], b_recv.at[t, 0], partner
+        ).start()
+
+    def second(t):
+        at = t * whole
+        if t == 0:
+            loads[5].wait()
+        landed(r0.at[pl.ds(at, whole)], b_recv.at[t, 0])
+        part = min(32, whole)
+
+        @pl.loop(0, whole // part)
+        def _(step):
+            some = pl.ds(at + step * part, part)
+            value = bucket[some] + r0[some]
+            bucket[some] = value
+            s1[some] = value.astype(BF16)
+
+        @pl.loop(1, half)
+        def _(o):
+            other = lax.rem(pos + o, half)
+            remote(
+                s1.at[pl.ds(at + other * q, q)], r1.at[t, o - 1],
+                b_send.at[t, 1], b_recv.at[t, 1], in_space(other * 2 + core),
+            ).start()
+
+    def third(t):
+        if half > 1:
+            landed(r1.at[t], b_recv.at[t, 1])
+        own = pl.ds(t * whole + pos * q, q)
+        value = bucket[own]
+        for o in range(1, half):
+            value = value + r1[t, o - 1].astype(F32)
+        bucket[own] = value
+        s2[t] = value.astype(BF16)
+
+        @pl.loop(1, n)
+        def _(o):
+            other = lax.rem(dp + o, n)
+            remote(
+                s2.at[t, pl.ds(other * e, e)], r2.at[t, o - 1], b_send.at[t, 2], b_recv.at[t, 2], in_dp(other)
+            ).start()
+
+    def fourth(t):
+        landed(r2.at[t], b_recv.at[t, 2])
+        value = bucket[pl.ds(t * whole + pos * q + dp * e, e)]
+        for o in range(1, n):
+            value = value + r2[t, o - 1].astype(F32)
+        own = gath.at[pl.ds(near + t * whole + pos * q + dp * e, e)]
+        own[...] = value.astype(BF16)
+
+        @pl.loop(1, n)
+        def _(o):
+            remote(own, own, b_send.at[t, 3], b_recv.at[t, 3], in_dp(lax.rem(dp + o, n))).start()
+
+    def share(t, chip):
+        return gath.at[pl.ds(near + t * whole + chip * q, q)]
+
+    def fifth(t):
+        landed(gath.at[pl.ds(0, (n - 1) * e)], b_recv.at[t, 3])
+
+        @pl.loop(1, half)
+        def _(o):
+            other = lax.rem(pos + o, half)
+            remote(share(t, pos), share(t, pos), b_send.at[t, 4], c_recv.at[t, o - 1], in_space(other * 2 + core)).start()
+
+        remote(share(t, pos), share(t, pos), b_send.at[t, 5], b_recv.at[t, 5], partner).start()
+
+    def sixth(t):
+        @pl.loop(1, half)
+        def _(o):
+            chip = lax.rem(pos + half - o, half)
+            landed(share(t, chip), c_recv.at[t, o - 1])
+            remote(share(t, chip), share(t, chip), b_send.at[t, 5], b_recv.at[t, 5], partner).start()
+
     if n * m > 1:
         pl.semaphore_wait(barrier, m - 1 + n - 1)
+
+    def clear():
+        for field in (cotf, actf, volf, pref):
+            for slot in (0, width_x + 1):
+                field[slot] = jnp.zeros(field.shape[1:], BF16)
+        gpart[...] = jnp.zeros(gpart.shape, F32)
+        blank(cotf)
+        blank(volf)
+        blank(pref)
+
+    def load_cot():
+        loads[0].wait()
+        center(raw_cot, cotf, c2)
         for c, (low, high) in enumerate(raw_cuts):
             send_halo(cotf, low, high, c)
-        remote(bucket_hbm.at[pl.ds(pl.multiple_of(far, h), h), :], r0, b_send.at[0], b_recv.at[0], partner).start()
-    blank(cotf)
-    blank(volf)
-    blank(pref)
-    loads[1].wait()
-    center(raw_vol, volf, c0)
-    if n * m > 1:
+
+    def load_vol():
+        loads[1].wait()
+        center(raw_vol, volf, c0)
         send_halo(volf, 0, width_x, 2 * pieces)
-    loads[2].wait()
-    spread(raw_act, actf, c1)
-    loads[3].wait()
-    weights(two_v, w_two, c1)
-    loads[4].wait()
-    weights(one_v, w_one, c0)
-    loads[5].wait()
-
-    part = min(256, h)
-    if m > 1:
-        landed(r0, b_recv.at[0])
-
-        @pl.loop(0, h // part)
-        def _(t):
-            at = pl.ds(t * part, part)
-            value = bucket[at, :] + r0[at, :]
-            bucket[at, :] = value
-            s1[at, :] = value.astype(BF16)
-
-        @pl.loop(1, half)
-        def _(o):
-            other = lax.rem(pos + o, half)
-            remote(
-                s1.at[pl.ds(pl.multiple_of(other * q, q), q), :], r1.at[o - 1],
-                b_send.at[1], b_recv.at[1], in_space(other * 2 + core),
-            ).start()
-
-    def third():
-        if half > 1:
-            landed(r1, b_recv.at[1])
-        own = pl.ds(pl.multiple_of(pos * q, q), q)
-        value = bucket[own, :]
-        for o in range(1, half):
-            value = value + r1[o - 1].astype(F32)
-        bucket[own, :] = value
-        s2[...] = value.astype(BF16)
-
-        @pl.loop(1, n)
-        def _(o):
-            other = lax.rem(dp + o, n)
-            remote(
-                s2.at[pl.ds(pl.multiple_of(other * e, e), e), :], r2.at[o - 1],
-                b_send.at[2], b_recv.at[2], in_dp(other),
-            ).start()
-
-    for c in range(pieces):
+
+    def load_act():
+        loads[2].wait()
+        spread(raw_act, actf, c1)
+
+    def load_weights():
+        loads[3].wait()
+        weights(two_v, w_two, c1)
+        loads[4].wait()
+        weights(one_v, w_one, c0)
+
+    def convolve_one(c):
         low, high = pre_cuts[c]
-        if m > 1:
-            have_halo(cotf, *raw_cuts[c], c)
+        have_halo(cotf, *raw_cuts[c], c)
 
         @pl.loop(0, (high - low) // COUNT)
         def _(step):
@@ -282,17 +329,26 @@
                 turned[x + u, c1 : 2 * c1, :] = value
                 turned[x + u, 2 * c1 :, :] = shifted(wide, -1).astype(BF16)
 
-        if m > 1:
-            send_halo(pref, low, high, pieces + c)
-            if c == 2:
-                third()
+        send_halo(pref, low, high, pieces + c)
+
+    def terms_two(c):
         kernel_terms(actf, cotf, 1, gpart, 0, *raw_cuts[c], UNROLL)
 
-    if m > 1:
+    def terms_one():
         have_halo(volf, 0, width_x, 2 * pieces)
-    kernel_terms(volf, turned, 0, gpart, 9 * c1, 0, width_x, UNROLL)
-
-    if m > 1:
+        kernel_terms(volf, turned, 0, gpart, 9 * c1, 0, width_x, UNROLL)
+
+    def convolve_two():
+        for c in range(pieces):
+            have_halo(pref, *pre_cuts[c], pieces + c)
+
+        @pl.loop(0, width_x // COUNT)
+        def _(step):
+            x = step * COUNT
+            for u, value in enumerate(convolved(pref, w_one, x, COUNT, c0)):
+                gin[x + u] = value.astype(BF16)
+
+    def gradients_cut():
         gsend[...] = gpart[...].astype(gsend.dtype)
 
         @pl.loop(1, m)
@@ -303,30 +359,7 @@
                 g_send.at[0], g_recv.at[0], in_space(other),
             ).start()
 
-        landed(r2, b_recv.at[2])
-        value = bucket[pl.ds(pl.multiple_of(pos * q + dp * e, e), e), :]
-        for o in range(1, n):
-            value = value + r2[o - 1].astype(F32)
-        own_rows = gath.at[pl.ds(pl.multiple_of(mine + dp * e, e), e), :]
-        own_rows[...] = value.astype(BF16)
-
-        @pl.loop(1, n)
-        def _(o):
-            remote(own_rows, own_rows, b_send.at[3], b_recv.at[3], in_dp(lax.rem(dp + o, n))).start()
-
-    def second(low, high):
-        @pl.loop(0, (high - low) // COUNT)
-        def _(step):
-            x = low + step * COUNT
-            for u, value in enumerate(convolved(pref, w_one, x, COUNT, c0)):
-                gin[x + u] = value.astype(BF16)
-
-    if m > 1:
-        for c in range(pieces):
-            have_halo(pref, *pre_cuts[c], pieces + c)
-    second(0, width_x)
-
-    if m > 1:
+    def gradients_swap():
         landed(grecv, g_recv.at[0])
         value = gpart[pl.ds(pl.multiple_of(sp * gr, gr), gr), :]
         for o in range(1, m):
@@ -337,18 +370,7 @@
         def _(o):
             remote(gx.at[dp], gx.at[dp], g_send.at[1], g_recv.at[1], in_dp(lax.rem(dp + o, n))).start()
 
-        def rows_of(chip):
-            return gath.at[pl.ds(pl.multiple_of(near + chip * q, q), q), :]
-
-        landed(gath.at[pl.ds(0, (n - 1) * e), :], b_recv.at[3])
-
-        @pl.loop(1, half)
-        def _(o):
-            other = lax.rem(pos + o, half)
-            remote(rows_of(pos), rows_of(pos), b_send.at[4], c_recv.at[o - 1], in_space(other * 2 + core)).start()
-
-        remote(rows_of(pos), rows_of(pos), b_send.at[5], b_recv.at[5], partner).start()
-
+    def gradients_join():
         landed(gx.at[pl.ds(0, n - 1)], g_recv.at[1])
         value = gx[0].astype(F32)
         for d in range(1, n):
@@ -360,26 +382,54 @@
         def _(o):
             remote(own_g, own_g, g_send.at[2], g_recv.at[2], in_space(lax.rem(sp + o, m))).start()
 
-        @pl.loop(1, half)
-        def _(o):
-            chip = lax.rem(pos + half - o, half)
-            landed(rows_of(chip), c_recv.at[o - 1])
-            remote(rows_of(chip), rows_of(chip), b_send.at[5], b_recv.at[5], partner).start()
-
+    first(0)
+    first(1)
+    load_cot()
+    second(0)
+    second(1)
+    clear()
+    load_vol()
+    load_act()
+    load_weights()
+    convolve_one(0)
+    terms_two(0)
+    convolve_one(1)
+    terms_two(1)
+    third(0)
+    convolve_one(2)
+    terms_two(2)
+    third(1)
+    convolve_one(3)
+    terms_two(3)
+    terms_one()
+    gradients_cut()
+    fourth(0)
+    fourth(1)
+    gradients_swap()
+    fifth(0)
+    fifth(1)
+    gradients_join()
+    convolve_two()
+    sixth(0)
+    sixth(1)
+
+    if m > 1:
         landed(gfull.at[pl.ds(0, (m - 1) * gr), :], g_recv.at[2])
-        landed(gath.at[pl.ds(0, h), :], b_recv.at[5])
+        for t in range(PARTS):
+            landed(gath.at[pl.ds(0, whole)], b_recv.at[t, 5])
 
         for c in range(pieces):
             sent_halo(cotf, *raw_cuts[c], c)
             sent_halo(pref, *pre_cuts[c], pieces + c)
         sent_halo(volf, 0, width_x, 2 * pieces)
-        landed(r0, b_send.at[0])
-        if half > 1:
-            landed(r1, b_send.at[1])
-            landed(gath.at[pl.ds(0, (half - 1) * q), :], b_send.at[4])
-        landed(r2, b_send.at[2])
-        landed(gath.at[pl.ds(0, (n - 1) * e), :], b_send.at[3])
-        landed(gath.at[pl.ds(0, h), :], b_send.at[5])
+        for t in range(PARTS):
+            landed(r0.at[pl.ds(0, whole)], b_send.at[t, 0])
+            if half > 1:
+                landed(r1.at[t], b_send.at[t, 1])
+                landed(gath.at[pl.ds(0, (half - 1) * q)], b_send.at[t, 4])
+            landed(r2.at[t], b_send.at[t, 2])
+            landed(gath.at[pl.ds(0, (n - 1) * e)], b_send.at[t, 3])
+            landed(gath.at[pl.ds(0, whole)], b_send.at[t, 5])
         landed(grecv, g_send.at[0])
         landed(gx.at[pl.ds(0, n - 1)], g_send.at[1])
         landed(gfull.at[pl.ds(0, (m - 1) * gr), :], g_send.at[2])
@@ -394,8 +444,8 @@
     copies = []
     for t in range(count):
         at = pl.ds(t * part, part)
-        bsum_v[at, :] = gath[at, :].astype(F32)
-        copies.append(pltpu.make_async_copy(bsum_v.at[at, :], bsum_hbm.at[at, :], sem.at[t]))
+        bsum_v[at] = gath[at].astype(F32)
+        copies.append(pltpu.make_async_copy(bsum_v.at[at], bsum_hbm.at[at], sem.at[t]))
         copies[-1].start()
     block = 16
     for t in range(width_x // block):
@@ -424,25 +474,28 @@
     rows = bucket.shape[0]
     half = max(m // 2, 1)
     h = rows // 2
-    q = h // half
+    q = h // PARTS // half
     e = q // n
     gr = GROWS // m
     wire = BF16
+    tile = (TILE, LANES)
     vmem = pltpu.VMEM
     dma = pltpu.SemaphoreType.DMA
     tall = width_x + 2
     scratch = [
         vmem((c0, width_x, width_y), BF16), vmem((c1, width_x, width_y), BF16), vmem((c2, width_x, width_y), BF16),
-        vmem((27, c0, c1), BF16), vmem((27, c1, c2), BF16), vmem((h, LANES), F32),
+        vmem((27, c0, c1), BF16), vmem((27, c1, c2), BF16), vmem((h, *tile), F32),
         vmem((tall, 3 * c2, LANES), BF16), vmem((tall, 3 * c1, LANES), BF16),
         vmem((tall, 3 * c0, LANES), BF16), vmem((tall, 3 * c1, LANES), BF16),
         vmem((width_x, 3 * c1, LANES), BF16),
         vmem((3 * c0, 9 * c1), BF16), vmem((3 * c1, 9 * c2), BF16),
-        vmem((h, LANES), F32), vmem((h, LANES), BF16),
-        vmem((max(half - 1, 1), q, LANES), BF16), vmem((q, LANES), BF16), vmem((max(n - 1, 1), e, LANES), BF16),
+        vmem((h, *tile), F32), vmem((h, *tile), BF16),
+        vmem((PARTS, max(half - 1, 1), q, *tile), BF16), vmem((PARTS, q, *tile), BF16),
+        vmem((PARTS, max(n - 1, 1), e, *tile), BF16),
         vmem((GROWS, LANES), F32), vmem((GROWS, LANES), wire), vmem((max(m - 1, 1), gr, LANES), wire),
         vmem((n, gr, LANES), wire),
-        dma((6,)), dma((9, 2)), dma((9, 2)), dma((6,)), dma((6,)), dma((max(half - 1, 1),)), dma((3,)), dma((3,)),
+        dma((6,)), dma((9, 2)), dma((9, 2)), dma((PARTS, 6)), dma((PARTS, 6)), dma((PARTS, max(half - 1, 1))),
+        dma((3,)), dma((3,)),
     ]
     hbm = pl.BlockSpec(memory_space=pltpu.HBM)
     local = pl.BlockSpec(memory_space=pltpu.VMEM)
@@ -453,7 +506,7 @@
         out_shape=(
             jax.ShapeDtypeStruct((width_x, c0, width_y), BF16),
             jax.ShapeDtypeStruct((GROWS, LANES), wire),
-            jax.ShapeDtypeStruct((rows, LANES), BF16),
+            jax.ShapeDtypeStruct((rows, *tile), BF16),
         ),
         in_specs=[hbm] * 6,
         out_specs=(local,) * 3,
@@ -471,13 +524,13 @@
             jax.ShapeDtypeStruct((c0, width_x, width_y), BF16),
             jax.ShapeDtypeStruct((27, c0, c1), F32),
             jax.ShapeDtypeStruct((27, c1, c2), F32),
-            jax.ShapeDtypeStruct((rows, LANES), F32),
+            jax.ShapeDtypeStruct((rows, *tile), F32),
         ),
         in_specs=[local] * 3,
         out_specs=(hbm,) * 4,
         scratch_shapes=[
             vmem((c0, width_x, width_y), BF16), vmem((27, c0, c1), F32), vmem((27, c1, c2), F32),
-            vmem((rows, LANES), F32), dma((11,)),
+            vmem((rows, *tile), F32), dma((11,)),
         ],
         compiler_params=pltpu.CompilerParams(vmem_limit_bytes=VMEM_LIMIT),
         cost_estimate=pl.CostEstimate(flops=0, bytes_accessed=5 << 20, transcendentals=0),
@@ -491,7 +544,7 @@
         n, m, scale,
         volume_in[0, 0], hidden_act[0, 0], out_cot[0, 0],
         kernel_one.reshape((27,) + kernel_one.shape[3:]), kernel_two.reshape((27,) + kernel_two.shape[3:]),
-        grad_bucket.reshape(-1, LANES),
+        grad_bucket.reshape(-1, TILE, LANES),
     )
     return (gin[None, None], g1.reshape(kernel_one.shape), g2.reshape(kernel_two.shape), bsum.reshape(-1))
 

time: 53.4 us -> 51.5 us (0.964)
  Pallas kernels: 52.7 us -> 50.7 us
    pallas_call x1, Pallas kernels: 50.9 us -> 49 us  [call(): pl.pallas_call(functools.partial(kernel, n, m, scale), out_shape=(jax.Sha...]
where the time goes in v3:
time: 51.5 us; the launch traced here: 51.4 us
  Pallas kernels  50.7 us (98%)
  between operations  0.64 us (1%)
    pallas_call x1, Pallas kernels, call(): pl.pallas_call(functools.partial(kernel, n, m, scale), out_shape=(jax.Sha...  49 us
    pallas_call x1, Pallas kernels, call(): pl.pallas_call(finish, out_shape=(jax.ShapeDtypeStruct((c0, width_x, widt...  1.76 us

profile of v3, /device:TPU:1, one launch (start us, length us, event | category | flops | bytes accessed | tf_op | source)
XLA Modules:
  0.0 51.4 jit_solution(13960122798316404891)
XLA Ops:
  0.6 49.0 %shard_map.93 = (bf16[64,16,128]{2,1,0:T(8,128)(2,1)S(1)}, bf16[512,128]{1,0:T(8,128)(2,1)S(1)}, bf16[512,8,128]{2,1,0:T(8,128)(2,1)S(1)}) custom-call(bf16[16,64,128]{2,1,0:T(8,128)(2,1)} %bitcast.15, bf16[32,64,128]{2,1,0:T(8,128)(2,1)} %bitcast.12, bf16[32,64,128]{2,1,0:T(8,128)(2,1)} %bitcast.13, bf16[27,16,32]{2,1,0:T(8,128)(2,1)} %bitcast.19, ...), custom_call_target="tpu_custom_call" | custom-call | flops 1358954496 | bytes 8388608 | tf_op jit(solution)/shard_map/pallas_call | solution.py:504
  49.6 1.8 %shard_map.94 = (bf16[16,64,128]{2,1,0:T(8,128)(2,1)}, f32[27,16,32]{2,1,0:T(8,128)}, f32[27,32,32]{2,1,0:T(8,128)}, f32[512,8,128]{2,1,0:T(8,128)}) custom-call(bf16[64,16,128]{2,1,0:T(8,128)(2,1)S(1)} %get-tuple-element.11.gin, bf16[512,128]{1,0:T(8,128)(2,1)S(1)} %get-tuple-element.12.gfull, bf16[512,8,128]{2,1,0:T(8,128)(2,1)S(1)} %get-tuple-element.13.gath), custom_call_target="tpu_custom_call" | custom-call | bytes 5242880 | tf_op jit(solution)/shard_map/pallas_call | solution.py:521

commit v4 on v3

--- a/solution.py
+++ b/solution.py
@@ -60,17 +60,19 @@
 
 
 def kernel_terms(left, right, offset, out, first, low, high, unroll):
+    @pl.loop(0, (high - low) // unroll)
+    def _(step):
+        add_terms(left, right, offset, out, first, low + step * unroll, unroll)
+
+
+def add_terms(left, right, offset, out, first, x, unroll):
     rows = 3 * left.shape[1]
     depth = right.shape[1]
-
-    @pl.loop(0, (high - low) // unroll)
-    def _(step):
-        x = low + step * unroll
-        a = jnp.concatenate([left[pl.ds(x + u, 3)].reshape(rows, LANES) for u in range(unroll)], axis=1)
-        b = jnp.concatenate([right[x + u + offset] for u in range(unroll)], axis=1)
-        out[first : first + rows, :depth] += lax.dot_general(
-            a, b, (((1,), (1,)), ((), ())), preferred_element_type=F32
-        )
+    a = jnp.concatenate([left[pl.ds(x + u, 3)].reshape(rows, LANES) for u in range(unroll)], axis=1)
+    b = jnp.concatenate([right[x + u + offset] for u in range(unroll)], axis=1)
+    out[first : first + rows, :depth] += lax.dot_general(
+        a, b, (((1,), (1,)), ((), ())), preferred_element_type=F32
+    )
 
 
 def kernel(
@@ -93,7 +95,7 @@
     whole = h // PARTS
     q = whole // half
     e = q // n
-    gr = GROWS // m
+    gr = GROWS // n
     near, far = core * h, (1 - core) * h
     partner = (dp, sp + 1 - 2 * core)
 
@@ -320,6 +322,7 @@
         @pl.loop(0, (high - low) // COUNT)
         def _(step):
             x = low + step * COUNT
+            add_terms(actf, cotf, 1, gpart, 0, x, COUNT)
             for u, value in enumerate(convolved(cotf, w_two, x, COUNT, c1)):
                 slope = jnp.where(actf[x + u + 1, c1 : 2 * c1, :].astype(F32) > 0, 1.0, 0.2)
                 value = (value * slope).astype(BF16)
@@ -331,9 +334,6 @@
 
         send_halo(pref, low, high, pieces + c)
 
-    def terms_two(c):
-        kernel_terms(actf, cotf, 1, gpart, 0, *raw_cuts[c], UNROLL)
-
     def terms_one():
         have_halo(volf, 0, width_x, 2 * pieces)
         kernel_terms(volf, turned, 0, gpart, 9 * c1, 0, width_x, UNROLL)
@@ -351,36 +351,36 @@
     def gradients_cut():
         gsend[...] = gpart[...].astype(gsend.dtype)
 
-        @pl.loop(1, m)
-        def _(o):
-            other = lax.rem(sp + o, m)
+        @pl.loop(1, n)
+        def _(o):
+            other = lax.rem(dp + o, n)
             remote(
                 gsend.at[pl.ds(pl.multiple_of(other * gr, gr), gr), :], grecv.at[o - 1],
-                g_send.at[0], g_recv.at[0], in_space(other),
+                g_send.at[0], g_recv.at[0], in_dp(other),
             ).start()
 
     def gradients_swap():
         landed(grecv, g_recv.at[0])
-        value = gpart[pl.ds(pl.multiple_of(sp * gr, gr), gr), :]
-        for o in range(1, m):
+        value = gpart[pl.ds(pl.multiple_of(dp * gr, gr), gr), :]
+        for o in range(1, n):
             value = value + grecv[o - 1].astype(F32)
-        gx[dp] = value.astype(gx.dtype)
+        gx[sp] = value.astype(gx.dtype)
+
+        @pl.loop(1, m)
+        def _(o):
+            remote(gx.at[sp], gx.at[sp], g_send.at[1], g_recv.at[1], in_space(lax.rem(sp + o, m))).start()
+
+    def gradients_join():
+        landed(gx.at[pl.ds(0, m - 1)], g_recv.at[1])
+        value = gx[0].astype(F32)
+        for d in range(1, m):
+            value = value + gx[d].astype(F32)
+        own_g = gfull.at[pl.ds(pl.multiple_of(dp * gr, gr), gr), :]
+        own_g[...] = (value * scale).astype(gfull.dtype)
 
         @pl.loop(1, n)
         def _(o):
-            remote(gx.at[dp], gx.at[dp], g_send.at[1], g_recv.at[1], in_dp(lax.rem(dp + o, n))).start()
-
-    def gradients_join():
-        landed(gx.at[pl.ds(0, n - 1)], g_recv.at[1])
-        value = gx[0].astype(F32)
-        for d in range(1, n):
-            value = value + gx[d].astype(F32)
-        own_g = gfull.at[pl.ds(pl.multiple_of(sp * gr, gr), gr), :]
-        own_g[...] = (value * scale).astype(gfull.dtype)
-
-        @pl.loop(1, m)
-        def _(o):
-            remote(own_g, own_g, g_send.at[2], g_recv.at[2], in_space(lax.rem(sp + o, m))).start()
+            remote(own_g, own_g, g_send.at[2], g_recv.at[2], in_dp(lax.rem(dp + o, n))).start()
 
     first(0)
     first(1)
@@ -392,15 +392,11 @@
     load_act()
     load_weights()
     convolve_one(0)
-    terms_two(0)
     convolve_one(1)
-    terms_two(1)
     third(0)
     convolve_one(2)
-    terms_two(2)
     third(1)
     convolve_one(3)
-    terms_two(3)
     terms_one()
     gradients_cut()
     fourth(0)
@@ -414,7 +410,7 @@
     sixth(1)
 
     if m > 1:
-        landed(gfull.at[pl.ds(0, (m - 1) * gr), :], g_recv.at[2])
+        landed(gfull.at[pl.ds(0, (n - 1) * gr), :], g_recv.at[2])
         for t in range(PARTS):
             landed(gath.at[pl.ds(0, whole)], b_recv.at[t, 5])
 
@@ -431,8 +427,8 @@
             landed(gath.at[pl.ds(0, (n - 1) * e)], b_send.at[t, 3])
             landed(gath.at[pl.ds(0, whole)], b_send.at[t, 5])
         landed(grecv, g_send.at[0])
-        landed(gx.at[pl.ds(0, n - 1)], g_send.at[1])
-        landed(gfull.at[pl.ds(0, (m - 1) * gr), :], g_send.at[2])
+        landed(gx.at[pl.ds(0, m - 1)], g_send.at[1])
+        landed(gfull.at[pl.ds(0, (n - 1) * gr), :], g_send.at[2])
 
 
 def finish(gin, gfull, gath, gin_hbm, g1_hbm, g2_hbm, bsum_hbm, gin_v, g1_v, g2_v, bsum_v, sem):
@@ -476,7 +472,7 @@
     h = rows // 2
     q = h // PARTS // half
     e = q // n
-    gr = GROWS // m
+    gr = GROWS // n
     wire = BF16
     tile = (TILE, LANES)
     vmem = pltpu.VMEM
@@ -492,8 +488,8 @@
         vmem((h, *tile), F32), vmem((h, *tile), BF16),
         vmem((PARTS, max(half - 1, 1), q, *tile), BF16), vmem((PARTS, q, *tile), BF16),
         vmem((PARTS, max(n - 1, 1), e, *tile), BF16),
-        vmem((GROWS, LANES), F32), vmem((GROWS, LANES), wire), vmem((max(m - 1, 1), gr, LANES), wire),
-        vmem((n, gr, LANES), wire),
+        vmem((GROWS, LANES), F32), vmem((GROWS, LANES), wire), vmem((max(n - 1, 1), gr, LANES), wire),
+        vmem((m, gr, LANES), wire),
         dma((6,)), dma((9, 2)), dma((9, 2)), dma((PARTS, 6)), dma((PARTS, 6)), dma((PARTS, max(half - 1, 1))),
         dma((3,)), dma((3,)),
     ]

time: 51.5 us -> 51.1 us (level)
  no operation moved by 1% of the time
where the time goes in v4:
time: 51.1 us; the launch traced here: 51 us
  Pallas kernels  50.3 us (98%)
  between operations  0.64 us (1%)
    pallas_call x1, Pallas kernels, call(): pl.pallas_call(functools.partial(kernel, n, m, scale), out_shape=(jax.Sha...  48.6 us
    pallas_call x1, Pallas kernels, call(): pl.pallas_call(finish, out_shape=(jax.ShapeDtypeStruct((c0, width_x, widt...  1.76 us

profile of v4, /device:TPU:1, one launch (start us, length us, event | category | flops | bytes accessed | tf_op | source)
XLA Modules:
  0.0 51.0 jit_solution(394819702197456692)
XLA Ops:
  0.6 48.6 %shard_map.93 = (bf16[64,16,128]{2,1,0:T(8,128)(2,1)S(1)}, bf16[512,128]{1,0:T(8,128)(2,1)S(1)}, bf16[512,8,128]{2,1,0:T(8,128)(2,1)S(1)}) custom-call(bf16[16,64,128]{2,1,0:T(8,128)(2,1)} %bitcast.15, bf16[32,64,128]{2,1,0:T(8,128)(2,1)} %bitcast.12, bf16[32,64,128]{2,1,0:T(8,128)(2,1)} %bitcast.13, bf16[27,16,32]{2,1,0:T(8,128)(2,1)} %bitcast.19, ...), custom_call_target="tpu_custom_call" | custom-call | flops 1358954496 | bytes 8388608 | tf_op jit(solution)/shard_map/pallas_call | solution.py:500
  49.2 1.8 %shard_map.94 = (bf16[16,64,128]{2,1,0:T(8,128)(2,1)}, f32[27,16,32]{2,1,0:T(8,128)}, f32[27,32,32]{2,1,0:T(8,128)}, f32[512,8,128]{2,1,0:T(8,128)}) custom-call(bf16[64,16,128]{2,1,0:T(8,128)(2,1)S(1)} %get-tuple-element.11.gin, bf16[512,128]{1,0:T(8,128)(2,1)S(1)} %get-tuple-element.12.gfull, bf16[512,8,128]{2,1,0:T(8,128)(2,1)S(1)} %get-tuple-element.13.gath), custom_call_target="tpu_custom_call" | custom-call | bytes 5242880 | tf_op jit(solution)/shard_map/pallas_call | solution.py:517

commit v5 on v4

--- a/solution.py
+++ b/solution.py
@@ -13,7 +13,7 @@
 BF16 = jnp.bfloat16
 LANES = 128
 GROWS = 512
-UNROLL = 16
+UNROLL = 32
 COUNT = 8
 PARTS = 2
 TILE = 8

time: 51.1 us -> 51 us (level)
  no operation moved by 1% of the time
where the time goes in v5:
time: 51 us; the launch traced here: 50.9 us
  Pallas kernels  50.3 us (99%)
  between operations  0.64 us (1%)
    pallas_call x1, Pallas kernels, call(): pl.pallas_call(functools.partial(kernel, n, m, scale), out_shape=(jax.Sha...  48.5 us
    pallas_call x1, Pallas kernels, call(): pl.pallas_call(finish, out_shape=(jax.ShapeDtypeStruct((c0, width_x, widt...  1.76 us

profile of v5, /device:TPU:1, one launch (start us, length us, event | category | flops | bytes accessed | tf_op | source)
XLA Modules:
  0.0 50.9 jit_solution(4882481623401403375)
XLA Ops:
  0.6 48.5 %shard_map.93 = (bf16[64,16,128]{2,1,0:T(8,128)(2,1)S(1)}, bf16[512,128]{1,0:T(8,128)(2,1)S(1)}, bf16[512,8,128]{2,1,0:T(8,128)(2,1)S(1)}) custom-call(bf16[16,64,128]{2,1,0:T(8,128)(2,1)} %bitcast.15, bf16[32,64,128]{2,1,0:T(8,128)(2,1)} %bitcast.12, bf16[32,64,128]{2,1,0:T(8,128)(2,1)} %bitcast.13, bf16[27,16,32]{2,1,0:T(8,128)(2,1)} %bitcast.19, ...), custom_call_target="tpu_custom_call" | custom-call | flops 1358954496 | bytes 8388608 | tf_op jit(solution)/shard_map/pallas_call | solution.py:500
  49.1 1.8 %shard_map.94 = (bf16[16,64,128]{2,1,0:T(8,128)(2,1)}, f32[27,16,32]{2,1,0:T(8,128)}, f32[27,32,32]{2,1,0:T(8,128)}, f32[512,8,128]{2,1,0:T(8,128)}) custom-call(bf16[64,16,128]{2,1,0:T(8,128)(2,1)S(1)} %get-tuple-element.11.gin, bf16[512,128]{1,0:T(8,128)(2,1)S(1)} %get-tuple-element.12.gfull, bf16[512,8,128]{2,1,0:T(8,128)(2,1)S(1)} %get-tuple-element.13.gath), custom_call_target="tpu_custom_call" | custom-call | bytes 5242880 | tf_op jit(solution)/shard_map/pallas_call | solution.py:517
